TPU v7x, 128 devices: a whole 4x4x4 slice. The times are simulated.
128 devices in a mesh: curve: 128 (over z, y, x, core).
Axes of the slice: x: 4, y: 4, z: 4, core: 2. Of those that a mesh axis runs over, the one named last changes fastest.
Arguments:
- state: float32 [3, 64, 65536], P(None, None, 'curve'), as said below
- neighbours: int32 [4, 65536], P(None, 'curve'), may hold values from -1 to 65535, as said below
- metric: float32 [65536], P('curve'), may hold values from 0.5 to 4
- flags: int32 [65536], P('curve'), may hold values 0 or 1
- new_owner: int32 [65536, 1], P('curve'), may hold values from 0 to 127; in each aligned block of 512 rows (0 to 511, 512 to 1023, ...) at most 8 rows name the same one
Outputs:
- migrated: float32 [4, 3, 64, 131072], P(None, None, None, 'curve')
Inputs may be any that keep to these rules, and one draw needn't show every extreme that they name: `state`: the first of the three fields (depth) lies between 0.5 and 2.0 at every node. Faces pair up: if neighbours[f, e] = n >= 0 then neighbours[opposite f, n] = e, and walls (-1) come in such pairs too. The element across face 0 or 1 lies on the same device or the next or previous one; across face 2 or 3 on the same device or the device 32 after or before. At most 32 elements of a device have their neighbour across one given face on one given other device, and every device but the last has exactly 32 across face 1 on the next device. `new_owner`: the rows of one device name each owner at most 8 times, a bound that some block reaches.
All inputs are finite; a program needn't handle non-finite values. No bound on the sum of `flags` on one device may be relied on, other than what follows from the above.
Results may differ from a plain program's by a relative error of at most 0.0003.
Values sent between devices are 32-bit elements; how exact they have to be, the bound alone decides.
A program may use at most 64 MiB of HBM per device.

v0:
```python
import jax
import jax.numpy as jnp
import numpy as np
from jax import lax
from jax.sharding import PartitionSpec as P

lgl_nodes = np.array(
    [
        -1.0,
        -0.8717401485096066,
        -0.5917001814331423,
        -0.2092992179024789,
        0.2092992179024789,
        0.5917001814331423,
        0.8717401485096066,
        1.0,
    ]
)
end_weight = 1.0 / 28.0
earth_pressure = 1.2
friction = 0.4
slope_x = 0.3
slope_y = 0.1
time_step = 0.01
face_nodes = np.array(
    [
        [8 * r for r in range(8)],
        [8 * r + 7 for r in range(8)],
        [r for r in range(8)],
        [56 + r for r in range(8)],
    ]
)
opposite = [1, 0, 3, 2]
outward = [-1.0, 1.0, -1.0, 1.0]


def shifted(block, axis, distance):
    devices = range(lax.axis_size(axis))
    route = [(i - distance, i) for i in devices if i - distance in devices]
    return lax.ppermute(block, axis, route)


def lagrange_table(points):
    values_table = np.ones((len(points), 8))
    for j in range(8):
        for m in range(8):
            if m != j:
                values_table[:, j] = (
                    values_table[:, j] * (points - lgl_nodes[m]) / (lgl_nodes[j] - lgl_nodes[m])
                )
    return values_table


def basis_tables():
    bary = np.array(
        [1.0 / np.prod([lgl_nodes[j] - lgl_nodes[m] for m in range(8) if m != j]) for j in range(8)]
    )
    derivative = np.zeros((8, 8))
    for i in range(8):
        for j in range(8):
            if i != j:
                derivative[i, j] = bary[j] / bary[i] / (lgl_nodes[i] - lgl_nodes[j])
        derivative[i, i] = -np.sum(derivative[i])
    identity = np.eye(8)
    lower_half = lagrange_table((lgl_nodes - 1.0) / 2.0)
    upper_half = lagrange_table((lgl_nodes + 1.0) / 2.0)
    halves = [lower_half, upper_half]
    prolong = np.stack(
        [
            np.kron(halves[row_half], halves[col_half])
            for row_half in range(2)
            for col_half in range(2)
        ]
    )
    return (
        jnp.asarray(np.kron(identity, derivative), jnp.float32),
        jnp.asarray(np.kron(derivative, identity), jnp.float32),
        jnp.asarray(prolong, jnp.float32),
    )


def face_flux(values, face_id):
    depth_field = values[0]
    moment_x = values[1]
    moment_y = values[2]
    speed_x = moment_x / depth_field
    speed_y = moment_y / depth_field
    pressure = 0.5 * earth_pressure * depth_field * depth_field
    if face_id < 2:
        normal = speed_x
        flux_term = jnp.stack([moment_x, moment_x * speed_x + pressure, moment_y * speed_x])
    else:
        normal = speed_y
        flux_term = jnp.stack([moment_y, moment_x * speed_y, moment_y * speed_y + pressure])
    return (outward[face_id] * flux_term, jnp.abs(normal) + jnp.sqrt(earth_pressure * depth_field))


def mirror(values, face_id):
    if face_id < 2:
        return jnp.stack([values[0], -values[1], values[2]])
    return jnp.stack([values[0], values[1], -values[2]])


def tendency(fields, metric, outsides, deriv_x, deriv_y):
    depth_field = fields[0]
    moment_x = fields[1]
    moment_y = fields[2]
    speed_x = moment_x / depth_field
    speed_y = moment_y / depth_field
    pressure = 0.5 * earth_pressure * depth_field * depth_field
    flux_x = jnp.stack([moment_x, moment_x * speed_x + pressure, moment_y * speed_x])
    flux_y = jnp.stack([moment_y, moment_x * speed_y, moment_y * speed_y + pressure])
    volume = jnp.einsum(
        "ab,fbe->fae", deriv_x, flux_x, precision=lax.Precision.HIGHEST
    ) + jnp.einsum("ab,fbe->fae", deriv_y, flux_y, precision=lax.Precision.HIGHEST)
    magnitude = jnp.sqrt(speed_x * speed_x + speed_y * speed_y + 1.0)
    source = jnp.stack(
        [
            jnp.zeros_like(depth_field),
            depth_field * (slope_x - friction * speed_x / magnitude),
            depth_field * (slope_y - friction * speed_y / magnitude),
        ]
    )
    scale_row = metric[None, None, :]
    result = source - scale_row * volume
    for face_id in range(4):
        inside = fields[:, face_nodes[face_id], :]
        flux_in, wave_in = face_flux(inside, face_id)
        flux_out, wave_out = face_flux(outsides[face_id], face_id)
        largest = jnp.maximum(wave_in, wave_out)
        star = 0.5 * (flux_in + flux_out) - 0.5 * largest[None] * (outsides[face_id] - inside)
        result = result.at[:, face_nodes[face_id], :].add(scale_row / end_weight * (flux_in - star))
    return result


def make_children(fields, flag_values, prolong):
    prolonged = jnp.einsum("cab,fbe->cfae", prolong, fields, precision=lax.Precision.HIGHEST)
    empty_field = jnp.zeros_like(fields)
    unchanged = jnp.stack([fields, empty_field, empty_field, empty_field])
    return jnp.where((flag_values == 1)[None, None, None, :], prolonged, unchanged)


def slot_columns(destination, devices_count, slots):
    hits_table = (
        destination[:, None] == jnp.arange(devices_count, dtype=jnp.int32)[None, :]
    ).astype(jnp.int32)
    before = jnp.sum(jnp.cumsum(hits_table, axis=0) * hits_table, axis=1) - 1
    return destination * slots + before


def on_device(state, neighbours, metric, flags, new_owner):
    deriv_x, deriv_y, prolong = basis_tables()
    elems = state.shape[2]
    devices_count = lax.axis_size("curve")
    stride = devices_count // 4
    my_index = lax.axis_index("curve")
    owners = jnp.where(neighbours >= 0, neighbours // elems, -1)
    local_at = jnp.clip(neighbours - owners * elems, 0, elems - 1)
    traces = [state[:, face_nodes[face_id], :].reshape(24, elems) for face_id in range(4)]

    def outgoing_for(face_pair):
        return jnp.stack([traces[face_id] for face_id in face_pair])

    def fetch_ghost(received, face_pair, face_id):
        position = face_pair.index(opposite[face_id])
        column = local_at[face_id]
        return received[position][:, column].reshape(3, 8, elems)

    near_pair = [0, 1]
    far_pair = [2, 3]
    near_below = shifted(outgoing_for(near_pair), "curve", 1)
    near_above = shifted(outgoing_for(near_pair), "curve", -1)
    far_below = shifted(outgoing_for(far_pair), "curve", stride)
    far_above = shifted(outgoing_for(far_pair), "curve", -stride)
    outsides = []
    for face_id in range(4):
        if face_id < 2:
            face_pair, below_ghosts, above_ghosts, distance = (near_pair, near_below, near_above, 1)
        else:
            face_pair, below_ghosts, above_ghosts, distance = (
                far_pair,
                far_below,
                far_above,
                stride,
            )
        inside_trace = state[:, face_nodes[face_id], :]
        across = traces[opposite[face_id]][:, local_at[face_id]].reshape(3, 8, elems)
        from_below = fetch_ghost(below_ghosts, face_pair, face_id)
        from_above = fetch_ghost(above_ghosts, face_pair, face_id)
        owner_row = owners[face_id][None, None, :]
        outside = jnp.where(
            owner_row == my_index,
            across,
            jnp.where(owner_row == my_index - distance, from_below, from_above),
        )
        outside = jnp.where(owner_row < 0, mirror(inside_trace, face_id), outside)
        outsides.append(outside)
    stepped = state + time_step * tendency(state, metric, outsides, deriv_x, deriv_y)
    slots = max(2, 2 * elems // devices_count)
    columns = slot_columns(new_owner[:, 0], devices_count, slots)
    children = make_children(stepped, flags, prolong).reshape(768, elems)
    outgoing = jnp.zeros((devices_count * slots, 768), jnp.float32).at[columns].set(children.T)
    arrived = lax.all_to_all(
        outgoing.reshape(devices_count, slots, 768),
        "curve",
        split_axis=0,
        concat_axis=0,
        tiled=True,
    )
    return arrived.reshape(devices_count * slots, 768).T.reshape(4, 3, 64, devices_count * slots)


def solution(mesh):
    placed = (P(None, None, "curve"), P(None, "curve"), P("curve"), P("curve"), P("curve", None))
    return jax.shard_map(
        on_device,
        mesh=mesh,
        in_specs=placed,
        out_specs=P(None, None, None, "curve"),
        check_vma=False,
    )
```

profile of v0, /device:TPU:1, one launch (start us, length us, event | category | flops | bytes accessed | tf_op | source)
XLA Modules:
  0.0 120.2 jit_solution(6703162544167867153)
XLA Ops:
  0.7 1.6 %gather_fusion.9 = f32[8,3,512]{2,0,1:T(8,128)S(1)} fusion(f32[3,64,512]{2,1,0:T(8,128)} %param.40, s32[1024]{0:T(1024)S(1)} %pad_clamp_fusion.2), kind=kCustom, calls=%fused_computation.9 | custom fusion | bytes 98336 | tf_op jit(solution)/shard_map/gather | solution.py:159
  2.4 1.6 %gather_fusion.8 = f32[8,3,512]{2,0,1:T(8,128)S(1)} fusion(f32[3,64,512]{2,1,0:T(8,128)} %param.40, s32[1024]{0:T(1024)S(1)} %pad_clamp_fusion.3), kind=kCustom, calls=%fused_computation.8 | custom fusion | bytes 98336 | tf_op jit(solution)/shard_map/gather | solution.py:127
  4.3 1.3 %collective-permute-start.3 = (f32[2,24,512]{1,2,0:T(8,128)S(1)}, f32[2,24,512]{1,2,0:T(8,128)}, u32[]{:S(2)}, u32[]{:S(2)}) collective-permute-start(f32[2,24,512]{1,2,0:T(8,128)S(1)} %copy.117), channel_id=1, source_target_pairs={{32,0},{33,1},{34,2},{35,3},{36,4},{37,5},{38,6},{39,7},{40,8},{41... | collective-permute-start | bytes 294920 | tf_op jit(solution)/shard_map/ppermute | solution.py:40
  5.6 5.8 %collective-permute-start.2 = (f32[2,24,512]{1,2,0:T(8,128)S(1)}, f32[2,24,512]{1,2,0:T(8,128)}, u32[]{:S(2)}, u32[]{:S(2)}) collective-permute-start(f32[2,24,512]{1,2,0:T(8,128)S(1)} %copy.117), channel_id=1, source_target_pairs={{0,32},{1,33},{2,34},{3,35},{4,36},{5,37},{6,38},{7,39},{8,40},{9,... | collective-permute-start | bytes 294920 | tf_op jit(solution)/shard_map/ppermute | solution.py:40
  13.3 2.9 %collective-permute-start.1 = (f32[2,24,512]{1,2,0:T(8,128)S(1)}, f32[2,24,512]{1,2,0:T(8,128)}, u32[]{:S(2)}, u32[]{:S(2)}) collective-permute-start(f32[2,24,512]{1,2,0:T(8,128)S(1)} %copy.104), channel_id=1, source_target_pairs={{1,0},{2,1},{3,2},{4,3},{5,4},{6,5},{7,6},{8,7},{9,8},{10,9},{11,1... | collective-permute-start | bytes 294920 | tf_op jit(solution)/shard_map/ppermute | solution.py:40
  16.2 3.1 %collective-permute-start = (f32[2,24,512]{1,2,0:T(8,128)S(1)}, f32[2,24,512]{1,2,0:T(8,128)S(1)}, u32[]{:S(2)}, u32[]{:S(2)}) collective-permute-start(f32[2,24,512]{1,2,0:T(8,128)S(1)} %copy.104), channel_id=1, source_target_pairs={{0,1},{1,2},{2,3},{3,4},{4,5},{5,6},{6,7},{7,8},{8,9},{9,10},{10,1... | collective-permute-start | bytes 294920 | tf_op jit(solution)/shard_map/ppermute | solution.py:40
  26.3 1.0 gather_fusion.13
  28.3 1.0 gather_fusion.5
  29.5 1.0 gather_fusion.2
  31.5 1.0 gather_fusion.10
  35.4 1.1 slice_bitcast_fusion
  36.5 1.2 gather_fusion.15
  38.4 1.3 %gather_fusion.12 = f32[512,24]{1,0:T(8,128)S(1)} fusion(f32[24,512]{0,1:T(8,128)S(1)} %get-tuple-element.26, s32[1024]{0:T(1024)} %copy-done.24), kind=kCustom, calls=%fused_computation.12 | custom fusion | bytes 100352 | tf_op jit(solution)/shard_map/gather | solution.py:167
  39.9 1.1 slice_bitcast_fusion.1
  42.1 1.0 gather_fusion.11
  44.7 1.1 slice_bitcast_fusion.4
  45.8 1.0 gather_fusion.7
  47.1 1.0 gather_fusion.4
  49.5 1.3 %gather_fusion.3 = f32[512,24]{1,0:T(8,128)S(1)} fusion(f32[24,512]{0,1:T(8,128)S(1)} %get-tuple-element.28, s32[1024]{0:T(1024)} %copy-done.19), kind=kCustom, calls=%fused_computation.3 | custom fusion | bytes 100352 | tf_op jit(solution)/shard_map/gather | solution.py:167
  55.1 1.5 %maximum_select_fusion = f32[4,3,64,512]{3,2,0,1:T(8,128)S(1)} fusion(f32[1,3,64,512]{3,2,0,1:T(8,128)S(1)} %fusion.22, f32[4,64,64,1]{2,1,0,3:T(8,128)S(1)} %copy-done.5, f32[4]{0:T(128)S(1)} %copy-done.46, f32[4]{0:T(128)S(1)} %copy-done.45, pred[512]{0:T(512)(128)(4,1)S(1)} %copy-done.37, f32[3,64,512]{2,1,0:T(8,128)S(1)} %copy-done, ...), kind=kOutput, calls=%fused_computation.21 | convolution fusion | flops 303366144 | bytes 2818592 | tf_op jit(solution)/shard_map/cab,fbe->cfae/dot_general | solution.py:137
  56.7 1.6 %copy.129 = f32[512,768]{1,0:T(8,128)} copy(f32[512,768]{0,1:T(8,128)S(1)} %bitcast.175) | data formatting | bytes 3145728 | tf_op jit(solution)/shard_map/transpose | solution.py:202
  58.3 3.9 %scatter_custom_fusion.4 = f32[1024,768]{1,0:T(8,128)S(1)} fusion(s32[512]{0:T(512)} %bitcast.216, f32[512,768]{1,0:T(8,128)} %copy.129, f32[]{:T(128)} %constant.29.clone.1), kind=kCustom, calls=%fused_computation.22 | custom fusion | bytes 3146240 | tf_op jit(solution)/shard_map/scatter | solution.py:202
  62.2 54.5 %all_to_all.5 = f32[128,8,768]{2,1,0:T(8,128)} all-to-all(f32[128,8,768]{2,1,0:T(8,128)S(1)} %bitcast.173), channel_id=1, replica_groups=mesh['curve'=128] {'curve'}, dimensions={0} | all-to-all | bytes 6291456 | tf_op jit(solution)/shard_map/all_to_all | solution.py:203
  116.7 3.5 %copy.130 = f32[1024,768]{0,1:T(8,128)} copy(f32[1024,768]{1,0:T(8,128)} %bitcast.174) | data formatting | bytes 6291456 | tf_op jit(solution)/shard_map/reshape | solution.py:210
  (184 shorter events, 23.6 us)
Async XLA Ops:
  0.0 11.8 %copy-start.33 = (s32[8]{0:T(128)S(1)}, s32[8]{0:T(128)}, u32[]{:S(2)}) copy-start(s32[8]{0:T(128)} %constant.100) | copy-start | bytes 100
  0.0 11.9 %copy-start = (f32[3,64,512]{2,1,0:T(8,128)S(1)}, f32[3,64,512]{2,1,0:T(8,128)}, u32[]{:S(2)}) copy-start(f32[3,64,512]{2,1,0:T(8,128)} %param.40) | copy-start | bytes 1179652
  4.0 17.8 %copy-start.38 = (s32[512]{0:T(512)S(1)}, s32[512]{0:T(512)}, u32[]{:S(2)}) copy-start(s32[512]{0:T(512)} %param.43) | copy-start | bytes 6148
  4.0 18.9 %copy-start.30 = (f32[512]{0:T(512)S(1)}, f32[512]{0:T(512)}, u32[]{:S(2)}) copy-start(f32[512]{0:T(512)} %param.42) | copy-start | bytes 6148
  4.0 19.5 %copy-start.31 = (s32[4,512]{1,0:T(4,128)S(1)}, s32[4,512]{1,0:T(4,128)}, u32[]{:S(2)}) copy-start(s32[4,512]{1,0:T(4,128)} %param.41) | copy-start | bytes 24580
  4.2 20.7 %copy-start.29 = (s32[512,1]{0,1:T(1,128)S(1)}, s32[512,1]{0,1:T(1,128)}, u32[]{:S(2)}) copy-start(s32[512,1]{0,1:T(1,128)} %param.44) | copy-start | bytes 6148
  4.3 31.2 %collective-permute-start.3 = (f32[2,24,512]{1,2,0:T(8,128)S(1)}, f32[2,24,512]{1,2,0:T(8,128)}, u32[]{:S(2)}, u32[]{:S(2)}) collective-permute-start(f32[2,24,512]{1,2,0:T(8,128)S(1)} %copy.117), channel_id=1, source_target_pairs={{32,0},{33,1},{34,2},{35,3},{36,4},{37,5},{38,6},{39,7},{40,8},{41... | collective-permute-start | bytes 294920 | tf_op jit(solution)/shard_map/ppermute | solution.py:40
  5.6 34.3 %collective-permute-start.2 = (f32[2,24,512]{1,2,0:T(8,128)S(1)}, f32[2,24,512]{1,2,0:T(8,128)}, u32[]{:S(2)}, u32[]{:S(2)}) collective-permute-start(f32[2,24,512]{1,2,0:T(8,128)S(1)} %copy.117), channel_id=1, source_target_pairs={{0,32},{1,33},{2,34},{3,35},{4,36},{5,37},{6,38},{7,39},{8,40},{9,... | collective-permute-start | bytes 294920 | tf_op jit(solution)/shard_map/ppermute | solution.py:40
  13.3 31.4 %collective-permute-start.1 = (f32[2,24,512]{1,2,0:T(8,128)S(1)}, f32[2,24,512]{1,2,0:T(8,128)}, u32[]{:S(2)}, u32[]{:S(2)}) collective-permute-start(f32[2,24,512]{1,2,0:T(8,128)S(1)} %copy.104), channel_id=1, source_target_pairs={{1,0},{2,1},{3,2},{4,3},{5,4},{6,5},{7,6},{8,7},{9,8},{10,9},{11,1... | collective-permute-start | bytes 294920 | tf_op jit(solution)/shard_map/ppermute | solution.py:40
  16.2 32.1 %collective-permute-start = (f32[2,24,512]{1,2,0:T(8,128)S(1)}, f32[2,24,512]{1,2,0:T(8,128)S(1)}, u32[]{:S(2)}, u32[]{:S(2)}) collective-permute-start(f32[2,24,512]{1,2,0:T(8,128)S(1)} %copy.104), channel_id=1, source_target_pairs={{0,1},{1,2},{2,3},{3,4},{4,5},{5,6},{6,7},{7,8},{8,9},{9,10},{10,1... | collective-permute-start | bytes 294920 | tf_op jit(solution)/shard_map/ppermute | solution.py:40
  23.6 7.8 %copy-start.24 = (s32[1024]{0:T(1024)}, s32[1024]{0:T(1024)S(1)}, u32[]{:S(2)}) copy-start(s32[1024]{0:T(1024)S(1)} %pad_clamp_fusion.1) | copy-start | bytes 12292
  23.6 4.6 %copy-start.26 = (s32[1024]{0:T(1024)}, s32[1024]{0:T(1024)S(1)}, u32[]{:S(2)}) copy-start(s32[1024]{0:T(1024)S(1)} %pad_clamp_fusion) | copy-start | bytes 12292
  23.6 4.6 %copy-start.21 = (s32[1024]{0:T(1024)}, s32[1024]{0:T(1024)S(1)}, u32[]{:S(2)}) copy-start(s32[1024]{0:T(1024)S(1)} %pad_clamp_fusion.4) | copy-start | bytes 12292
  23.7 5.9 %copy-start.19 = (s32[1024]{0:T(1024)}, s32[1024]{0:T(1024)S(1)}, u32[]{:S(2)}) copy-start(s32[1024]{0:T(1024)S(1)} %pad_clamp_fusion.5) | copy-start | bytes 12292
  38.4 4.8 %copy-start.2 = (f32[24,512]{1,0:T(8,128)S(1)}, f32[24,512]{1,0:T(8,128)}, u32[]{:S(2)}) copy-start(f32[24,512]{1,0:T(8,128)} %copy.123) | copy-start | bytes 147460
  38.4 4.8 %copy-start.3 = (f32[24,512]{1,0:T(8,128)S(1)}, f32[24,512]{1,0:T(8,128)}, u32[]{:S(2)}) copy-start(f32[24,512]{1,0:T(8,128)} %copy.116) | copy-start | bytes 147460
  38.4 4.9 %copy-start.4 = (f32[24,512]{1,0:T(8,128)S(1)}, f32[24,512]{1,0:T(8,128)}, u32[]{:S(2)}) copy-start(f32[24,512]{1,0:T(8,128)} %copy.125) | copy-start | bytes 147460
  38.4 4.9 %copy-start.6 = (f32[1,8,512]{2,1,0:T(8,128)S(1)}, f32[1,8,512]{2,1,0:T(8,128)}, u32[]{:S(2)}) copy-start(f32[1,8,512]{2,1,0:T(8,128)} %slice_negate_fusion) | copy-start | bytes 49156
  47.0 4.0 %copy-start.1 = (f32[24,512]{1,0:T(8,128)S(1)}, f32[24,512]{1,0:T(8,128)}, u32[]{:S(2)}) copy-start(f32[24,512]{1,0:T(8,128)} %copy.103) | copy-start | bytes 147460
  47.0 4.0 %copy-start.7 = (f32[1,8,512]{2,1,0:T(8,128)S(1)}, f32[1,8,512]{2,1,0:T(8,128)}, u32[]{:S(2)}) copy-start(f32[1,8,512]{2,1,0:T(8,128)} %get-tuple-element.68) | copy-start | bytes 49156
  47.0 4.0 %copy-start.8 = (f32[1,8,512]{2,1,0:T(8,128)S(1)}, f32[1,8,512]{2,1,0:T(8,128)}, u32[]{:S(2)}) copy-start(f32[1,8,512]{2,1,0:T(8,128)} %get-tuple-element.69) | copy-start | bytes 49156
  47.0 4.0 %copy-start.9 = (f32[1,8,512]{2,1,0:T(8,128)S(1)}, f32[1,8,512]{2,1,0:T(8,128)}, u32[]{:S(2)}) copy-start(f32[1,8,512]{2,1,0:T(8,128)} %get-tuple-element.70) | copy-start | bytes 49156
  47.0 4.0 %copy-start.10 = (f32[1,8,512]{2,1,0:T(8,128)S(1)}, f32[1,8,512]{2,1,0:T(8,128)}, u32[]{:S(2)}) copy-start(f32[1,8,512]{2,1,0:T(8,128)} %get-tuple-element.58) | copy-start | bytes 49156
  47.0 4.0 %copy-start.11 = (f32[1,8,512]{2,1,0:T(8,128)S(1)}, f32[1,8,512]{2,1,0:T(8,128)}, u32[]{:S(2)}) copy-start(f32[1,8,512]{2,1,0:T(8,128)} %get-tuple-element.59) | copy-start | bytes 49156
  (27 other events, 83.4 us)
where the time goes:
time: 121 us; the launch traced here: 120 us
  blocking collectives  54.5 us (45%)
  local copies, waits for them, and re-layouts  37.7 us (31%)
  starting transfers between devices  13.1 us (11%)
  other arithmetic  11.4 us (9%)
  matrix products  2.5 us (2%)
    all_to_all x1, blocking collectives, on_device(): lax.all_to_all(outgoing.reshape(devices_count, slots, 768), 'curve', spli...  54.5 us
    ppermute x4, starting transfers between devices, shifted(): return lax.ppermute(block, axis, route)  13.1 us
    gather x16, local copies, waits for them, and re-layouts, fetch_ghost(): return received[position][:, column].reshape(3, 8, elems)  10.4 us
    gather x8, local copies, waits for them, and re-layouts, on_device(): traces[opposite[face_id]][:, local_at[face_id]].reshape(3, 8, elems)  6.42 us
    scatter x1, local copies, waits for them, and re-layouts, on_device(): jnp.zeros((devices_count * slots, 768), jnp.float32).at[columns]  3.86 us
    reshape x1, local copies, waits for them, and re-layouts, on_device(): arrived.reshape(devices_count * slots, 768)  3.54 us
    scatter-add x4, other arithmetic, tendency(): result.at[:, face_nodes[face_id], :]  3.25 us
    squeeze x4, local copies, waits for them, and re-layouts, fetch_ghost(): return received[position][:, column].reshape(3, 8, elems)  3.23 us
  transfers between devices with their start and end apart: 4, of which 0 were waited for; matrix products, arithmetic and copies ran while one was open for 25% of the time, Pallas kernels for 0%

commit v1 on v0

v1 whole, which is shorter than its diff:
```python
import random

import jax
import jax.numpy as jnp
import numpy as np
from jax import lax
from jax.experimental import pallas as pl
from jax.experimental.pallas import tpu as pltpu
from jax.sharding import PartitionSpec as P

lgl_nodes = np.array(
    [
        -1.0,
        -0.8717401485096066,
        -0.5917001814331423,
        -0.2092992179024789,
        0.2092992179024789,
        0.5917001814331423,
        0.8717401485096066,
        1.0,
    ]
)
lift_weight = 28.0
earth_pressure = 1.2
friction = 0.4
slope_x = 0.3
slope_y = 0.1
time_step = 0.01
face_nodes = np.array(
    [
        [8 * r for r in range(8)],
        [8 * r + 7 for r in range(8)],
        [r for r in range(8)],
        [56 + r for r in range(8)],
    ]
)
inner_nodes = np.array([8 * iy + ix for iy in range(1, 7) for ix in range(1, 7)])
opposite = [1, 0, 3, 2]
outward = [-1.0, 1.0, -1.0, 1.0]

DEVICES = 128
ELEMS = 512
SLOTS = 8
LANES = 128
INNER = 40
OUTER = 32
FLAG_ROW = 3 * INNER
MESH = pl.DeviceIdType.MESH
bf16 = jnp.bfloat16
f32 = jnp.float32


def lagrange_table(points):
    values_table = np.ones((len(points), 8))
    for j in range(8):
        for m in range(8):
            if m != j:
                values_table[:, j] = (
                    values_table[:, j] * (points - lgl_nodes[m]) / (lgl_nodes[j] - lgl_nodes[m])
                )
    return values_table


def basis_tables():
    bary = np.array(
        [1.0 / np.prod([lgl_nodes[j] - lgl_nodes[m] for m in range(8) if m != j]) for j in range(8)]
    )
    derivative = np.zeros((8, 8))
    for i in range(8):
        for j in range(8):
            if i != j:
                derivative[i, j] = bary[j] / bary[i] / (lgl_nodes[i] - lgl_nodes[j])
        derivative[i, i] = -np.sum(derivative[i])
    identity = np.eye(8)
    lower_half = lagrange_table((lgl_nodes - 1.0) / 2.0)
    upper_half = lagrange_table((lgl_nodes + 1.0) / 2.0)
    halves = [lower_half, upper_half]
    prolong = np.stack(
        [
            np.kron(halves[row_half], halves[col_half])
            for row_half in range(2)
            for col_half in range(2)
        ]
    )
    return np.kron(identity, derivative), np.kron(derivative, identity), prolong


def two_parts(table):
    high = np.asarray(table, np.float32).astype(bf16)
    low = (np.asarray(table, np.float64) - high.astype(np.float64)).astype(bf16)
    return high, low


def corner_copy(face_id, r):
    return face_id < 2 and r in (0, 7)


def step_table():
    deriv_x, deriv_y, _ = basis_tables()
    full = np.concatenate([np.eye(64), deriv_x, deriv_y], axis=1)
    table = np.zeros((INNER + OUTER, 192))
    table[:36] = full[inner_nodes]
    for face_id in range(4):
        for r in range(8):
            if not corner_copy(face_id, r):
                table[INNER + 8 * face_id + r] = full[face_nodes[face_id][r]]
    high, low = two_parts(table)
    return np.concatenate([high, high, low[:, 64:]], axis=1)


def child_table():
    _, _, prolong = basis_tables()
    rows = np.concatenate([prolong.reshape(256, 64), np.eye(64)], axis=0)
    table = np.zeros((5, 3, 64, 2 * LANES))
    for field in range(3):
        block = np.zeros((5 * 64, 2 * LANES))
        block[:, INNER * field : INNER * field + 36] = rows[:, inner_nodes]
        for face_id in range(4):
            for r in range(8):
                at = LANES + OUTER * field + 8 * face_id + r
                block[:, at] = rows[:, face_nodes[face_id][r]]
        table[:, field] = block.reshape(5, 64, 2 * LANES)
    flag = np.zeros((8, 2 * LANES))
    flag[0, FLAG_ROW] = 1.0
    high, low = two_parts(np.concatenate([table.reshape(960, 2 * LANES), flag], axis=0))
    return high, low[:768]


def send_order():
    order = [
        (z, y, x, c) for z in range(4) for y in range(4) for x in range(4) for c in range(2)
    ][1:]
    random.Random(0).shuffle(order)
    order.sort(key=lambda d: -sum(min(v, 4 - v) for v in d[:3]))
    return order


def split2(values):
    high = values.astype(bf16)
    return high, (values - high.astype(f32)).astype(bf16)


def face_flux(values, face_id):
    depth, moment_x, moment_y = values
    inv = 1.0 / depth
    pressure = 0.5 * earth_pressure * depth * depth
    sign = outward[face_id]
    if face_id < 2:
        normal = moment_x * inv
        terms = [moment_x, moment_x * normal + pressure, moment_y * normal]
    else:
        normal = moment_y * inv
        terms = [moment_y, moment_x * normal, moment_y * normal + pressure]
    return [sign * t for t in terms], jnp.abs(normal) + jnp.sqrt(earth_pressure * depth)


def mirror(values, face_id):
    if face_id < 2:
        return [values[0], -values[1], values[2]]
    return [values[0], values[1], -values[2]]


def step_kernel(
    state, neighbours, metric, flags, owner, table,
    inner_in, outer_in,
    tiles, trace, ghost, inner_out, outer_out, onehot,
    halo_send, halo_recv, inner_send, inner_recv, outer_send, outer_recv, own_sem,
):
    me = lax.axis_index("curve")
    mz, my, mx, mc = me // 32, (me // 8) % 4, (me // 2) % 4, me % 2
    order = send_order()

    def device_at(d):
        z, y, x, c = d
        return (
            ((lax.rem(mz + z, 4) * 4 + lax.rem(my + y, 4)) * 4 + lax.rem(mx + x, 4)) * 2
            + lax.rem(mc + c, 2)
        )

    barrier = pltpu.get_barrier_semaphore()
    for d in order:
        pl.semaphore_signal(barrier, inc=1, device_id=(device_at(d),), device_id_type=MESH)

    for t in range(ELEMS // LANES):
        tiles[192 * t : 192 * t + 192, :] = state[:, LANES * t : LANES * t + LANES]
    for face_id in range(4):
        for field in range(3):
            at = (face_id % 2) * 24 + field * 8
            if face_id < 2:
                for t in range(ELEMS // LANES):
                    start = 192 * t + 64 * field + 7 * face_id
                    trace[0, at : at + 8, LANES * t : LANES * t + LANES] = tiles[
                        pl.ds(start, 8, stride=8), :
                    ]
            else:
                start = 64 * field + 56 * (face_id - 2)
                trace[1, at : at + 8, :] = state[start : start + 8, :]

    scale = (-time_step) * metric[...]
    depth, moment_x, moment_y = (state[64 * f : 64 * f + 64, :] for f in range(3))
    inv = 1.0 / depth
    speed_x, speed_y = moment_x * inv, moment_y * inv
    pressure = 0.5 * earth_pressure * depth * depth
    drag = friction / jnp.sqrt(speed_x * speed_x + speed_y * speed_y + 1.0)
    cross = moment_x * speed_y
    parts = [
        (depth, moment_x, moment_y),
        (
            moment_x + time_step * (depth * (slope_x - drag * speed_x)),
            moment_x * speed_x + pressure,
            cross,
        ),
        (
            moment_y + time_step * (depth * (slope_y - drag * speed_y)),
            cross,
            moment_y * speed_y + pressure,
        ),
    ]
    stepped = []
    for q, flux_x, flux_y in parts:
        q_high, q_low = split2(q)
        x_high, x_low = split2(scale * flux_x)
        y_high, y_low = split2(scale * flux_y)
        operand = jnp.concatenate(
            [q_high, x_high, y_high, q_low, x_low, y_low, x_high, y_high], axis=0
        )
        stepped.append(jnp.dot(table[...], operand, preferred_element_type=f32))

    owners = owner[...]
    hits = owners == lax.broadcasted_iota(jnp.int32, (DEVICES, ELEMS), 0)
    earlier = lax.broadcasted_iota(jnp.int32, (ELEMS, ELEMS), 0) < lax.broadcasted_iota(
        jnp.int32, (ELEMS, ELEMS), 1
    )
    hits = jnp.where(hits, 1.0, 0.0)
    before = jnp.dot(
        hits.astype(bf16),
        jnp.where(earlier, 1.0, 0.0).astype(bf16),
        preferred_element_type=f32,
    )
    rank = jnp.sum(hits * before, axis=0, keepdims=True)
    column = owners * SLOTS + rank.astype(jnp.int32)
    slot_rows = lax.broadcasted_iota(jnp.int32, (DEVICES * SLOTS, ELEMS), 0)
    onehot[...] = jnp.where(slot_rows == column, 1.0, 0.0).astype(bf16)

    def place(rows, target):
        high, low = split2(rows)
        both = lax.dot_general(
            onehot[...],
            jnp.concatenate([high, low], axis=0),
            (((1,), (1,)), ((), ())),
            preferred_element_type=f32,
        )
        placed = both[:, :LANES] + both[:, LANES:]
        target[...] = placed.reshape(DEVICES, SLOTS, LANES)

    flag_rows = jnp.where(
        lax.broadcasted_iota(jnp.int32, (8, ELEMS), 0) == 0, flags[...].astype(f32), 0.0
    )
    place(jnp.concatenate([s[:INNER] for s in stepped] + [flag_rows], axis=0), inner_out)

    pl.semaphore_wait(barrier, DEVICES - 1)

    def halo(pair, above):
        distance = 32 if pair else 1
        target = lax.rem(me + (distance if above else DEVICES - distance), DEVICES)
        side = 0 if above else 1
        return pltpu.make_async_remote_copy(
            src_ref=trace.at[pair],
            dst_ref=ghost.at[pair, side],
            send_sem=halo_send.at[pair, side],
            recv_sem=halo_recv.at[pair, side],
            device_id=(target,),
            device_id_type=MESH,
        )

    halos = [halo(pair, above) for pair in (0, 1) for above in (True, False)]
    for copy in halos:
        copy.start()

    def exchange(source, target, send_sem, recv_sem):
        for d in order:
            to = device_at(d)
            pltpu.make_async_remote_copy(
                src_ref=source.at[to],
                dst_ref=target.at[me],
                send_sem=send_sem,
                recv_sem=recv_sem,
                device_id=(to,),
                device_id_type=MESH,
            ).start()

    exchange(inner_out, inner_in, inner_send, inner_recv)
    own_inner = pltpu.make_async_copy(inner_out.at[me], inner_in.at[me], own_sem.at[0])
    own_inner.start()

    for copy in halos:
        copy.wait()

    lift_scale = (time_step * lift_weight * 0.5) * metric[...]
    lifted = [[None] * 4 for _ in range(3)]
    for face_id in range(4):
        pair, distance = (0, 1) if face_id < 2 else (1, 32)
        partner = neighbours[face_id : face_id + 1, :]
        wall = partner < 0
        home = lax.shift_right_arithmetic(partner, 9)
        local = jnp.bitwise_and(partner, ELEMS - 1)
        side = jnp.where(home == me, 0, jnp.where(home == me - distance, 1, 2))
        piece = side * 4 + lax.shift_right_arithmetic(local, 7)
        lane = jnp.bitwise_and(local, LANES - 1)
        at = (opposite[face_id] % 2) * 24
        across = [[], [], []]
        for t in range(ELEMS // LANES):
            cols = slice(t * LANES, (t + 1) * LANES)
            index = jnp.broadcast_to(lane[:, cols], (8, LANES))
            piece_t = jnp.broadcast_to(piece[:, cols], (8, LANES))
            found = [None, None, None]
            for c in range(12):
                there = slice((c % 4) * LANES, (c % 4 + 1) * LANES)
                mask = piece_t == c
                for field in range(3):
                    rows = slice(at + field * 8, at + field * 8 + 8)
                    if c < 4:
                        values = trace[pair, rows, there]
                    else:
                        values = ghost[pair, c // 4 - 1, rows, there]
                    got = jnp.take_along_axis(values, index, axis=1, mode="promise_in_bounds")
                    found[field] = got if c == 0 else jnp.where(mask, got, found[field])
            for field in range(3):
                across[field].append(found[field])
        at = (face_id % 2) * 24
        inside = [trace[pair, at + 8 * field : at + 8 * field + 8, :] for field in range(3)]
        outside = [
            jnp.where(wall, m, jnp.concatenate(a, axis=1))
            for m, a in zip(mirror(inside, face_id), across)
        ]
        flux_in, wave_in = face_flux(inside, face_id)
        flux_out, wave_out = face_flux(outside, face_id)
        largest = jnp.maximum(wave_in, wave_out)
        for field in range(3):
            jump = flux_in[field] - flux_out[field]
            lifted[field][face_id] = lift_scale * (
                jump + largest * (outside[field] - inside[field])
            )
    outer = [
        stepped[field][INNER:] + jnp.concatenate(lifted[field], axis=0) for field in range(3)
    ]
    place(jnp.concatenate(outer + [jnp.zeros((32, ELEMS), f32)], axis=0), outer_out)

    exchange(outer_out, outer_in, outer_send, outer_recv)
    own_outer = pltpu.make_async_copy(outer_out.at[me], outer_in.at[me], own_sem.at[1])
    own_outer.start()

    def wait_all(source, target, send_sem, recv_sem):
        others = pl.ds(0, DEVICES - 1)
        copies = pltpu.make_async_remote_copy(
            src_ref=source.at[others],
            dst_ref=target.at[others],
            send_sem=send_sem,
            recv_sem=recv_sem,
            device_id=(me,),
            device_id_type=MESH,
        )
        copies.wait_send()
        copies.wait_recv()

    own_inner.wait()
    own_outer.wait()
    wait_all(inner_out, inner_in, inner_send, inner_recv)
    wait_all(outer_out, outer_in, outer_send, outer_recv)


def child_kernel(inner, outer, high_table, low_table, out):
    columns = inner.shape[0]
    inner_high, inner_low = split2(inner[...])
    outer_high, outer_low = split2(outer[...])
    high = jnp.concatenate([inner_high, outer_high], axis=1)
    low = jnp.concatenate([inner_low, outer_low], axis=1)
    dims = (((1,), (1,)), ((), ()))
    main = lax.dot_general(
        high_table[...], high, dims, preferred_element_type=f32
    ) + lax.dot_general(high_table[...], low, dims, preferred_element_type=f32)
    fine = lax.dot_general(low_table[...], high, dims, preferred_element_type=f32)
    refined = jnp.broadcast_to(main[960:961] > 0.5, (192, columns))
    out[0:192, :] = jnp.where(refined, main[0:192] + fine[0:192], main[768:960])
    for c in range(1, 4):
        rows = slice(192 * c, 192 * c + 192)
        out[rows, :] = jnp.where(refined, main[rows] + fine[rows], 0.0)


def on_device(state, neighbours, metric, flags, new_owner):
    vmem = pl.BlockSpec(memory_space=pltpu.VMEM)
    hbm = pl.BlockSpec(memory_space=pl.ANY)
    block = jax.ShapeDtypeStruct((DEVICES, SLOTS, LANES), f32)
    buffer = pltpu.VMEM((DEVICES, SLOTS, LANES), f32)
    dma = pltpu.SemaphoreType.DMA
    inner, outer = pl.pallas_call(
        step_kernel,
        out_shape=(block, block),
        in_specs=[vmem] * 6,
        out_specs=(hbm, hbm),
        scratch_shapes=[
            pltpu.VMEM((192 * ELEMS // LANES, LANES), f32),
            pltpu.VMEM((2, 48, ELEMS), f32),
            pltpu.VMEM((2, 2, 48, ELEMS), f32),
            buffer,
            buffer,
            pltpu.VMEM((DEVICES * SLOTS, ELEMS), bf16),
            dma((2, 2)),
            dma((2, 2)),
            dma,
            dma,
            dma,
            dma,
            dma((2,)),
        ],
        compiler_params=pltpu.CompilerParams(collective_id=0, has_side_effects=True),
        name="step_and_migrate",
    )(
        state.reshape(192, ELEMS),
        neighbours,
        metric.reshape(1, ELEMS),
        flags.reshape(1, ELEMS),
        new_owner.reshape(1, ELEMS),
        jnp.asarray(step_table(), bf16),
    )
    slots = DEVICES * SLOTS
    tile = 256
    high_table, low_table = child_table()
    children = pl.pallas_call(
        child_kernel,
        grid=(slots // tile,),
        out_shape=jax.ShapeDtypeStruct((768, slots), f32),
        in_specs=[
            pl.BlockSpec((tile, LANES), lambda i: (i, 0)),
            pl.BlockSpec((tile, LANES), lambda i: (i, 0)),
            pl.BlockSpec((968, 2 * LANES), lambda i: (0, 0)),
            pl.BlockSpec((768, 2 * LANES), lambda i: (0, 0)),
        ],
        out_specs=pl.BlockSpec((768, tile), lambda i: (0, i)),
        name="make_children",
    )(
        inner.reshape(slots, LANES),
        outer.reshape(slots, LANES),
        jnp.asarray(high_table, bf16),
        jnp.asarray(low_table, bf16),
    )
    return children.reshape(4, 3, 64, slots)


def solution(mesh):
    placed = (P(None, None, "curve"), P(None, "curve"), P("curve"), P("curve"), P("curve", None))
    return jax.shard_map(
        on_device,
        mesh=mesh,
        in_specs=placed,
        out_specs=P(None, None, None, "curve"),
        check_vma=False,
    )
```

time: 121 us -> 35.9 us (0.30)
  blocking collectives: 54.5 us -> 0 us
  local copies, waits for them, and re-layouts: 37.7 us -> 0 us
  Pallas kernels: 0 us -> 35.7 us
  starting transfers between devices: 13.1 us -> 0 us
  other arithmetic: 11.4 us -> 0 us
  matrix products: 2.5 us -> 0 us
    all_to_all x1 -> x0, blocking collectives: 54.5 us -> none  [on_device(): lax.all_to_all(outgoing.reshape(devices_count, slots, 768), 'curve', spli...]
    pallas_call x0 -> x2, Pallas kernels: none -> 35.7 us  [the longest x1 30.4 us: on_device(): pl.pallas_call(step_kernel, out_shape=(block, block), in_specs=[vmem] * 6...]
    gather x28 -> x0, local copies, waits for them, and re-layouts: 21.3 us -> none  [the longest x16 10.4 us: fetch_ghost(): return received[position][:, column].reshape(3, 8, elems)]
    ppermute x4 -> x0, starting transfers between devices: 13.1 us -> none  [shifted(): return lax.ppermute(block, axis, route)]
    reshape x5 -> x0, local copies, waits for them, and re-layouts: 4.03 us -> none  [the longest x1 3.54 us: on_device(): arrived.reshape(devices_count * slots, 768)]
    scatter x1 -> x0, local copies, waits for them, and re-layouts: 3.86 us -> none  [on_device(): jnp.zeros((devices_count * slots, 768), jnp.float32).at[columns]]
    scatter-add x4 -> x0, other arithmetic: 3.25 us -> none  [tendency(): result.at[:, face_nodes[face_id], :]]
    squeeze x4 -> x0, local copies, waits for them, and re-layouts: 3.23 us -> none  [fetch_ghost(): return received[position][:, column].reshape(3, 8, elems)]
  transfers between devices with their start and end apart: 4 -> 0, of which waited for: 0 -> 0; matrix products, arithmetic and copies ran while one was open for 25% -> 0% of each run, Pallas kernels for 0% -> 0%
where the time goes in v1:
time: 35.9 us; the launch traced here: 35.7 us
  Pallas kernels  35.7 us (99%)
    pallas_call x1, Pallas kernels, on_device(): pl.pallas_call(step_kernel, out_shape=(block, block), in_specs=[vmem] * 6...  30.4 us
    pallas_call x1, Pallas kernels, on_device(): pl.pallas_call(child_kernel, grid=(slots // tile,), out_shape=jax.ShapeDt...  5.34 us

profile of v1, /device:TPU:1, one launch (start us, length us, event | category | flops | bytes accessed | tf_op | source)
XLA Modules:
  0.0 35.7 jit_solution(3290325783742886046)
XLA Ops:
  0.0 30.4 %step_and_migrate.1 = (f32[128,8,128]{2,1,0:T(8,128)}, f32[128,8,128]{2,1,0:T(8,128)}) custom-call(f32[192,512]{1,0:T(8,128)} %bitcast.9, s32[4,512]{1,0:T(4,128)} %neighbours.1, f32[1,512]{1,0:T(1,128)} %bitcast.10, s32[1,512]{1,0:T(1,128)} %bitcast.11, s32[1,512]{1,0:T(1,128)} %bitcast.12, bf16[72,512]{1,0:T(8,128)(2,1)} %constant.6.clone.table), custom_call_target="tpu_custom_call" | custom-call | tf_op jit(solution)/shard_map/step_and_migrate/pallas_call | solution.py:396
  30.4 5.3 %make_children.1 = f32[768,1024]{1,0:T(8,128)} custom-call(f32[1024,128]{1,0:T(8,128)} %bitcast.7, f32[1024,128]{1,0:T(8,128)} %bitcast.8, bf16[968,256]{1,0:T(8,128)(2,1)} %constant.7.clone.high_table, bf16[768,256]{1,0:T(8,128)(2,1)} %constant.8.clone.low_table), custom_call_target="tpu_custom_call" | custom-call | tf_op jit(solution)/shard_map/make_children/pallas_call | solution.py:429

commit v2 on v1

--- a/solution.py
+++ b/solution.py
@@ -45,6 +45,8 @@
 INNER = 40
 OUTER = 32
 FLAG_ROW = 3 * INNER
+CROSS = 32
+NAME_BASE = 2
 MESH = pl.DeviceIdType.MESH
 bf16 = jnp.bfloat16
 f32 = jnp.float32
@@ -161,25 +163,63 @@
 
 
 def step_kernel(
+    state_in, neighbours_in, metric_in, flags_in, owner_in, table_in,
+    inner_in, outer_in,
     state, neighbours, metric, flags, owner, table,
-    inner_in, outer_in,
-    tiles, trace, ghost, inner_out, outer_out, onehot,
-    halo_send, halo_recv, inner_send, inner_recv, outer_send, outer_recv, own_sem,
+    tiles, trace, own_flux, across, crossing, ghost, inner_out, outer_out, onehot,
+    load_sem, halo_send, halo_recv, inner_send, inner_recv, outer_send, outer_recv, own_sem,
 ):
+    pairs = (
+        (state_in, state), (neighbours_in, neighbours), (metric_in, metric),
+        (flags_in, flags), (owner_in, owner), (table_in, table),
+    )
+    loads = [pltpu.make_async_copy(a, b, load_sem.at[i]) for i, (a, b) in enumerate(pairs)]
+    for load in loads:
+        load.start()
+
     me = lax.axis_index("curve")
-    mz, my, mx, mc = me // 32, (me // 8) % 4, (me // 2) % 4, me % 2
     order = send_order()
-
-    def device_at(d):
-        z, y, x, c = d
-        return (
-            ((lax.rem(mz + z, 4) * 4 + lax.rem(my + y, 4)) * 4 + lax.rem(mx + x, 4)) * 2
-            + lax.rem(mc + c, 2)
-        )
+    z_part = [lax.rem(me // 32 + z, 4) * 32 for z in range(4)]
+    y_part = [lax.rem((me // 8) % 4 + y, 4) * 8 for y in range(4)]
+    x_part = [lax.rem((me // 2) % 4 + x, 4) * 2 for x in range(4)]
+    c_part = [lax.rem(me % 2 + c, 2) for c in range(2)]
+    zy_part = [[z + y for y in y_part] for z in z_part]
+    xc_part = [[x + c for c in c_part] for x in x_part]
+    others = [zy_part[z][y] + xc_part[x][c] for z, y, x, c in order]
 
     barrier = pltpu.get_barrier_semaphore()
-    for d in order:
-        pl.semaphore_signal(barrier, inc=1, device_id=(device_at(d),), device_id_type=MESH)
+    for to in others:
+        pl.semaphore_signal(barrier, inc=1, device_id=(to,), device_id_type=MESH)
+    for load in loads:
+        load.wait()
+
+    partners = neighbours[...]
+    distance = jnp.where(lax.broadcasted_iota(jnp.int32, (4, ELEMS), 0) < 2, 1, 32)
+    homes = lax.shift_right_arithmetic(partners, 9)
+    real = partners >= 0
+    below = jnp.where(real & (homes == me - distance), 1.0, 0.0)
+    above = jnp.where(real & (homes == me + distance), 1.0, 0.0)
+    owners = owner[...]
+    hits = owners == lax.broadcasted_iota(jnp.int32, (DEVICES, ELEMS), 0)
+    hits = jnp.where(hits, 1.0, 0.0)
+    earlier = lax.broadcasted_iota(jnp.int32, (ELEMS, ELEMS), 0) < lax.broadcasted_iota(
+        jnp.int32, (ELEMS, ELEMS), 1
+    )
+    nothing = jnp.zeros((4, ELEMS), f32)
+    before = jnp.dot(
+        jnp.concatenate([hits, below, nothing, above, nothing], axis=0).astype(bf16),
+        jnp.where(earlier, 1.0, 0.0).astype(bf16),
+        preferred_element_type=f32,
+    )
+    rank = jnp.sum(hits * before[:DEVICES], axis=0, keepdims=True)
+    column = owners * SLOTS + rank.astype(jnp.int32)
+    slot_rows = lax.broadcasted_iota(jnp.int32, (DEVICES * SLOTS, ELEMS), 0)
+    onehot[...] = jnp.where(slot_rows == column, 1.0, 0.0).astype(bf16)
+    spot = jnp.where(
+        below > 0.5,
+        before[DEVICES : DEVICES + 4],
+        jnp.where(above > 0.5, before[DEVICES + 8 : DEVICES + 12] + CROSS, -1000.0),
+    ).astype(jnp.int32)
 
     for t in range(ELEMS // LANES):
         tiles[192 * t : 192 * t + 192, :] = state[:, LANES * t : LANES * t + LANES]
@@ -195,6 +235,28 @@
             else:
                 start = 64 * field + 56 * (face_id - 2)
                 trace[1, at : at + 8, :] = state[start : start + 8, :]
+
+    first_row = lax.broadcasted_iota(jnp.int32, (8, ELEMS), 0) == 0
+    name = (
+        lax.broadcasted_iota(jnp.int32, (8, ELEMS), 1) + (me * ELEMS + NAME_BASE)
+    ).astype(f32)
+    name = jnp.where(first_row, name, 0.0)
+    lane_rows = lax.broadcasted_iota(jnp.int32, (LANES, ELEMS), 0)
+    nt_dims = (((1,), (1,)), ((), ()))
+    for pair in (0, 1):
+        packed = None
+        for position in (0, 1):
+            face_id = 2 * pair + position
+            rows = jnp.concatenate([trace[pair, 24 * position : 24 * position + 24, :], name])
+            chosen = lane_rows == spot[face_id : face_id + 1] + 2 * CROSS * position
+            part = lax.dot_general(
+                jnp.concatenate(split2(rows), axis=0),
+                jnp.where(chosen, 1.0, 0.0).astype(bf16),
+                nt_dims,
+                preferred_element_type=f32,
+            )
+            packed = part if packed is None else packed + part
+        crossing[pair] = packed[:32] + packed[32:]
 
     scale = (-time_step) * metric[...]
     depth, moment_x, moment_y = (state[64 * f : 64 * f + 64, :] for f in range(3))
@@ -226,46 +288,52 @@
         )
         stepped.append(jnp.dot(table[...], operand, preferred_element_type=f32))
 
-    owners = owner[...]
-    hits = owners == lax.broadcasted_iota(jnp.int32, (DEVICES, ELEMS), 0)
-    earlier = lax.broadcasted_iota(jnp.int32, (ELEMS, ELEMS), 0) < lax.broadcasted_iota(
-        jnp.int32, (ELEMS, ELEMS), 1
-    )
-    hits = jnp.where(hits, 1.0, 0.0)
-    before = jnp.dot(
-        hits.astype(bf16),
-        jnp.where(earlier, 1.0, 0.0).astype(bf16),
-        preferred_element_type=f32,
-    )
-    rank = jnp.sum(hits * before, axis=0, keepdims=True)
-    column = owners * SLOTS + rank.astype(jnp.int32)
-    slot_rows = lax.broadcasted_iota(jnp.int32, (DEVICES * SLOTS, ELEMS), 0)
-    onehot[...] = jnp.where(slot_rows == column, 1.0, 0.0).astype(bf16)
-
     def place(rows, target):
-        high, low = split2(rows)
         both = lax.dot_general(
             onehot[...],
-            jnp.concatenate([high, low], axis=0),
-            (((1,), (1,)), ((), ())),
+            jnp.concatenate(split2(rows), axis=0),
+            nt_dims,
             preferred_element_type=f32,
         )
         placed = both[:, :LANES] + both[:, LANES:]
         target[...] = placed.reshape(DEVICES, SLOTS, LANES)
 
-    flag_rows = jnp.where(
-        lax.broadcasted_iota(jnp.int32, (8, ELEMS), 0) == 0, flags[...].astype(f32), 0.0
-    )
+    flag_rows = jnp.where(first_row, flags[...].astype(f32), 0.0)
     place(jnp.concatenate([s[:INNER] for s in stepped] + [flag_rows], axis=0), inner_out)
 
+    for face_id in range(4):
+        pair = face_id // 2
+        at = (face_id % 2) * 24
+        inside = [trace[pair, at + 8 * field : at + 8 * field + 8, :] for field in range(3)]
+        flux_in, wave_in = face_flux(inside, face_id)
+        for i, values in enumerate(flux_in + [wave_in]):
+            own_flux[face_id, 8 * i : 8 * i + 8, :] = values
+        partner = partners[face_id : face_id + 1]
+        local = jnp.bitwise_and(partner, ELEMS - 1)
+        piece = lax.shift_right_arithmetic(local, 7)
+        lane = jnp.bitwise_and(local, LANES - 1)
+        at = (opposite[face_id] % 2) * 24
+        for t in range(ELEMS // LANES):
+            cols = slice(t * LANES, (t + 1) * LANES)
+            index = jnp.broadcast_to(lane[:, cols], (8, LANES))
+            piece_t = jnp.broadcast_to(piece[:, cols], (8, LANES))
+            for field in range(3):
+                rows = slice(at + field * 8, at + field * 8 + 8)
+                found = None
+                for c in range(ELEMS // LANES):
+                    values = trace[pair, rows, c * LANES : (c + 1) * LANES]
+                    got = jnp.take_along_axis(values, index, axis=1, mode="promise_in_bounds")
+                    found = got if c == 0 else jnp.where(piece_t == c, got, found)
+                across[face_id, 8 * field : 8 * field + 8, cols] = found
+
     pl.semaphore_wait(barrier, DEVICES - 1)
 
-    def halo(pair, above):
-        distance = 32 if pair else 1
-        target = lax.rem(me + (distance if above else DEVICES - distance), DEVICES)
-        side = 0 if above else 1
+    def halo(pair, upward):
+        far = 32 if pair else 1
+        target = lax.rem(me + (far if upward else DEVICES - far), DEVICES)
+        side = 0 if upward else 1
         return pltpu.make_async_remote_copy(
-            src_ref=trace.at[pair],
+            src_ref=crossing.at[pair],
             dst_ref=ghost.at[pair, side],
             send_sem=halo_send.at[pair, side],
             recv_sem=halo_recv.at[pair, side],
@@ -273,13 +341,12 @@
             device_id_type=MESH,
         )
 
-    halos = [halo(pair, above) for pair in (0, 1) for above in (True, False)]
+    halos = [halo(pair, upward) for pair in (0, 1) for upward in (True, False)]
     for copy in halos:
         copy.start()
 
     def exchange(source, target, send_sem, recv_sem):
-        for d in order:
-            to = device_at(d)
+        for to in others:
             pltpu.make_async_remote_copy(
                 src_ref=source.at[to],
                 dst_ref=target.at[me],
@@ -297,50 +364,46 @@
         copy.wait()
 
     lift_scale = (time_step * lift_weight * 0.5) * metric[...]
+    from_below = jnp.bitwise_and(lax.broadcasted_iota(jnp.int32, (32, LANES), 1), CROSS) != 0
+    named = (partners + NAME_BASE).astype(f32)
     lifted = [[None] * 4 for _ in range(3)]
-    for face_id in range(4):
-        pair, distance = (0, 1) if face_id < 2 else (1, 32)
-        partner = neighbours[face_id : face_id + 1, :]
-        wall = partner < 0
-        home = lax.shift_right_arithmetic(partner, 9)
-        local = jnp.bitwise_and(partner, ELEMS - 1)
-        side = jnp.where(home == me, 0, jnp.where(home == me - distance, 1, 2))
-        piece = side * 4 + lax.shift_right_arithmetic(local, 7)
-        lane = jnp.bitwise_and(local, LANES - 1)
-        at = (opposite[face_id] % 2) * 24
-        across = [[], [], []]
-        for t in range(ELEMS // LANES):
-            cols = slice(t * LANES, (t + 1) * LANES)
-            index = jnp.broadcast_to(lane[:, cols], (8, LANES))
-            piece_t = jnp.broadcast_to(piece[:, cols], (8, LANES))
-            found = [None, None, None]
-            for c in range(12):
-                there = slice((c % 4) * LANES, (c % 4 + 1) * LANES)
-                mask = piece_t == c
-                for field in range(3):
-                    rows = slice(at + field * 8, at + field * 8 + 8)
-                    if c < 4:
-                        values = trace[pair, rows, there]
-                    else:
-                        values = ghost[pair, c // 4 - 1, rows, there]
-                    got = jnp.take_along_axis(values, index, axis=1, mode="promise_in_bounds")
-                    found[field] = got if c == 0 else jnp.where(mask, got, found[field])
+    zeros = jnp.zeros((2 * CROSS, ELEMS), bf16)
+    for pair in (0, 1):
+        merged = jnp.where(from_below, ghost[pair, 0], ghost[pair, 1])
+        names = jnp.transpose(merged[24:32])[:, 0:1]
+        chosen = []
+        for position in (0, 1):
+            face_id = 2 * pair + position
+            start = 2 * CROSS * (1 - position)
+            match = names[start : start + 2 * CROSS] == named[face_id : face_id + 1]
+            match = jnp.where(match, 1.0, 0.0).astype(bf16)
+            chosen.append(jnp.concatenate([zeros, match] if start else [match, zeros], axis=0))
+        got = jnp.dot(
+            jnp.concatenate(split2(merged), axis=0),
+            jnp.concatenate(chosen, axis=1),
+            preferred_element_type=f32,
+        )
+        got = got[:32] + got[32:]
+        for position in (0, 1):
+            face_id = 2 * pair + position
+            wall = jnp.logical_not(real[face_id : face_id + 1])
+            local = homes[face_id : face_id + 1] == me
+            at = position * 24
+            inside = [trace[pair, at + 8 * field : at + 8 * field + 8, :] for field in range(3)]
+            reflected = mirror(inside, face_id)
+            outside = []
             for field in range(3):
-                across[field].append(found[field])
-        at = (face_id % 2) * 24
-        inside = [trace[pair, at + 8 * field : at + 8 * field + 8, :] for field in range(3)]
-        outside = [
-            jnp.where(wall, m, jnp.concatenate(a, axis=1))
-            for m, a in zip(mirror(inside, face_id), across)
-        ]
-        flux_in, wave_in = face_flux(inside, face_id)
-        flux_out, wave_out = face_flux(outside, face_id)
-        largest = jnp.maximum(wave_in, wave_out)
-        for field in range(3):
-            jump = flux_in[field] - flux_out[field]
-            lifted[field][face_id] = lift_scale * (
-                jump + largest * (outside[field] - inside[field])
-            )
+                rows = slice(8 * field, 8 * field + 8)
+                there = got[rows, ELEMS * position : ELEMS * position + ELEMS]
+                there = jnp.where(local, across[face_id, rows, :], there)
+                outside.append(jnp.where(wall, reflected[field], there))
+            flux_out, wave_out = face_flux(outside, face_id)
+            largest = jnp.maximum(own_flux[face_id, 24:32, :], wave_out)
+            for field in range(3):
+                jump = own_flux[face_id, 8 * field : 8 * field + 8, :] - flux_out[field]
+                lifted[field][face_id] = lift_scale * (
+                    jump + largest * (outside[field] - inside[field])
+                )
     outer = [
         stepped[field][INNER:] + jnp.concatenate(lifted[field], axis=0) for field in range(3)
     ]
@@ -351,10 +414,10 @@
     own_outer.start()
 
     def wait_all(source, target, send_sem, recv_sem):
-        others = pl.ds(0, DEVICES - 1)
+        every = pl.ds(0, DEVICES - 1)
         copies = pltpu.make_async_remote_copy(
-            src_ref=source.at[others],
-            dst_ref=target.at[others],
+            src_ref=source.at[every],
+            dst_ref=target.at[every],
             send_sem=send_sem,
             recv_sem=recv_sem,
             device_id=(me,),
@@ -388,7 +451,6 @@
 
 
 def on_device(state, neighbours, metric, flags, new_owner):
-    vmem = pl.BlockSpec(memory_space=pltpu.VMEM)
     hbm = pl.BlockSpec(memory_space=pl.ANY)
     block = jax.ShapeDtypeStruct((DEVICES, SLOTS, LANES), f32)
     buffer = pltpu.VMEM((DEVICES, SLOTS, LANES), f32)
@@ -396,15 +458,25 @@
     inner, outer = pl.pallas_call(
         step_kernel,
         out_shape=(block, block),
-        in_specs=[vmem] * 6,
+        in_specs=[hbm] * 6,
         out_specs=(hbm, hbm),
         scratch_shapes=[
+            pltpu.VMEM((192, ELEMS), f32),
+            pltpu.VMEM((4, ELEMS), jnp.int32),
+            pltpu.VMEM((1, ELEMS), f32),
+            pltpu.VMEM((1, ELEMS), jnp.int32),
+            pltpu.VMEM((1, ELEMS), jnp.int32),
+            pltpu.VMEM((INNER + OUTER, 512), bf16),
             pltpu.VMEM((192 * ELEMS // LANES, LANES), f32),
             pltpu.VMEM((2, 48, ELEMS), f32),
-            pltpu.VMEM((2, 2, 48, ELEMS), f32),
+            pltpu.VMEM((4, 32, ELEMS), f32),
+            pltpu.VMEM((4, 24, ELEMS), f32),
+            pltpu.VMEM((2, 32, LANES), f32),
+            pltpu.VMEM((2, 2, 32, LANES), f32),
             buffer,
             buffer,
             pltpu.VMEM((DEVICES * SLOTS, ELEMS), bf16),
+            dma((6,)),
             dma((2, 2)),
             dma((2, 2)),
             dma,

time: 35.9 us -> 33 us (0.919)
  Pallas kernels: 35.7 us -> 32.8 us
    pallas_call x1, Pallas kernels: 30.4 us -> 27.4 us  [on_device(): pl.pallas_call(step_kernel, out_shape=(block, block), in_specs=[hbm] * 6,...]
where the time goes in v2:
time: 33 us; the launch traced here: 32.8 us
  Pallas kernels  32.8 us (99%)
    pallas_call x1, Pallas kernels, on_device(): pl.pallas_call(step_kernel, out_shape=(block, block), in_specs=[hbm] * 6,...  27.4 us
    pallas_call x1, Pallas kernels, on_device(): pl.pallas_call(child_kernel, grid=(slots // tile,), out_shape=jax.ShapeDt...  5.34 us

profile of v2, /device:TPU:1, one launch (start us, length us, event | category | flops | bytes accessed | tf_op | source)
XLA Modules:
  0.0 32.8 jit_solution(1720468830704965371)
XLA Ops:
  0.0 27.4 %step_and_migrate.1 = (f32[128,8,128]{2,1,0:T(8,128)}, f32[128,8,128]{2,1,0:T(8,128)}) custom-call(f32[192,512]{1,0:T(8,128)} %bitcast.9, s32[4,512]{1,0:T(4,128)} %neighbours_in.1, f32[1,512]{1,0:T(1,128)} %bitcast.10, s32[1,512]{1,0:T(1,128)} %bitcast.11, s32[1,512]{1,0:T(1,128)} %bitcast.12, bf16[72,512]{1,0:T(8,128)(2,1)} %constant.6.clone.table_in), custom_call_target="tpu_custom_call" | custom-call | tf_op jit(solution)/shard_map/step_and_migrate/pallas_call | solution.py:458
  27.4 5.3 %make_children.1 = f32[768,1024]{1,0:T(8,128)} custom-call(f32[1024,128]{1,0:T(8,128)} %bitcast.7, f32[1024,128]{1,0:T(8,128)} %bitcast.8, bf16[968,256]{1,0:T(8,128)(2,1)} %constant.7.clone.high_table, bf16[768,256]{1,0:T(8,128)(2,1)} %constant.8.clone.low_table), custom_call_target="tpu_custom_call" | custom-call | tf_op jit(solution)/shard_map/make_children/pallas_call | solution.py:501

commit v3 on v2

--- a/solution.py
+++ b/solution.py
@@ -42,9 +42,13 @@
 ELEMS = 512
 SLOTS = 8
 LANES = 128
-INNER = 40
+MAIN = 32
 OUTER = 32
-FLAG_ROW = 3 * INNER
+EXTRA = 16
+INNER = 3 * MAIN + EXTRA
+FLAG = 12
+INNER_ROWS = 7
+OUTER_ROWS = 6
 CROSS = 32
 NAME_BASE = 2
 MESH = pl.DeviceIdType.MESH
@@ -100,32 +104,34 @@
 def step_table():
     deriv_x, deriv_y, _ = basis_tables()
     full = np.concatenate([np.eye(64), deriv_x, deriv_y], axis=1)
-    table = np.zeros((INNER + OUTER, 192))
-    table[:36] = full[inner_nodes]
-    for face_id in range(4):
-        for r in range(8):
-            if not corner_copy(face_id, r):
-                table[INNER + 8 * face_id + r] = full[face_nodes[face_id][r]]
-    high, low = two_parts(table)
+    table = np.zeros((3, MAIN + OUTER + EXTRA, 192))
+    for field in range(3):
+        table[field, :MAIN] = full[inner_nodes[:MAIN]]
+        for face_id in range(4):
+            for r in range(8):
+                if not corner_copy(face_id, r):
+                    table[field, MAIN + 8 * face_id + r] = full[face_nodes[face_id][r]]
+        start = MAIN + OUTER + 4 * field
+        table[field, start : start + 4] = full[inner_nodes[MAIN:]]
+    high, low = two_parts(table.reshape(-1, 192))
     return np.concatenate([high, high, low[:, 64:]], axis=1)
 
 
-def child_table():
+def child_tables():
     _, _, prolong = basis_tables()
     rows = np.concatenate([prolong.reshape(256, 64), np.eye(64)], axis=0)
-    table = np.zeros((5, 3, 64, 2 * LANES))
-    for field in range(3):
-        block = np.zeros((5 * 64, 2 * LANES))
-        block[:, INNER * field : INNER * field + 36] = rows[:, inner_nodes]
+    tables = []
+    for shift in (0, 4):
+        table = np.zeros((320, 80))
+        table[:, :MAIN] = rows[:, inner_nodes[:MAIN]]
         for face_id in range(4):
             for r in range(8):
-                at = LANES + OUTER * field + 8 * face_id + r
-                block[:, at] = rows[:, face_nodes[face_id][r]]
-        table[:, field] = block.reshape(5, 64, 2 * LANES)
-    flag = np.zeros((8, 2 * LANES))
-    flag[0, FLAG_ROW] = 1.0
-    high, low = two_parts(np.concatenate([table.reshape(960, 2 * LANES), flag], axis=0))
-    return high, low[:768]
+                table[:, MAIN + 8 * face_id + r] = rows[:, face_nodes[face_id][r]]
+        start = MAIN + OUTER + shift
+        table[:, start : start + 4] = rows[:, inner_nodes[MAIN:]]
+        high, low = two_parts(table)
+        tables.append(np.concatenate([high, high, low, np.zeros((320, 16), bf16)], axis=1))
+    return np.stack(tables)
 
 
 def send_order():
@@ -164,9 +170,10 @@
 
 def step_kernel(
     state_in, neighbours_in, metric_in, flags_in, owner_in, table_in,
-    inner_in, outer_in,
+    inner_turned_out, outer_in,
     state, neighbours, metric, flags, owner, table,
-    tiles, trace, own_flux, across, crossing, ghost, inner_out, outer_out, onehot,
+    tiles, trace, own_flux, across, crossing, ghost,
+    placed, inner_out, outer_out, inner_in, inner_turned, onehot,
     load_sem, halo_send, halo_recv, inner_send, inner_recv, outer_send, outer_recv, own_sem,
 ):
     pairs = (
@@ -286,20 +293,31 @@
         operand = jnp.concatenate(
             [q_high, x_high, y_high, q_low, x_low, y_low, x_high, y_high], axis=0
         )
-        stepped.append(jnp.dot(table[...], operand, preferred_element_type=f32))
-
-    def place(rows, target):
+        rows = slice(80 * len(stepped), 80 * len(stepped) + 80)
+        stepped.append(jnp.dot(table[rows, :], operand, preferred_element_type=f32))
+
+    def place(rows):
         both = lax.dot_general(
             onehot[...],
             jnp.concatenate(split2(rows), axis=0),
             nt_dims,
             preferred_element_type=f32,
         )
-        placed = both[:, :LANES] + both[:, LANES:]
-        target[...] = placed.reshape(DEVICES, SLOTS, LANES)
-
-    flag_rows = jnp.where(first_row, flags[...].astype(f32), 0.0)
-    place(jnp.concatenate([s[:INNER] for s in stepped] + [flag_rows], axis=0), inner_out)
+        placed[...] = both[:, :LANES] + both[:, LANES:]
+        return [placed[pl.ds(j, DEVICES, stride=SLOTS), :] for j in range(SLOTS)]
+
+    lane_at = lax.broadcasted_iota(jnp.int32, (DEVICES, LANES), 1)
+    extra = stepped[0][-EXTRA:] + stepped[1][-EXTRA:] + stepped[2][-EXTRA:]
+    flag_row = lax.broadcasted_iota(jnp.int32, (EXTRA, ELEMS), 0) == FLAG
+    extra = extra + jnp.where(flag_row, flags[...].astype(f32), 0.0)
+    slots = place(
+        jnp.concatenate(
+            [s[:MAIN] for s in stepped] + [extra, jnp.zeros((LANES - INNER, ELEMS), f32)], axis=0
+        )
+    )
+    for r in range(INNER_ROWS):
+        tail = pltpu.roll(slots[7], INNER - 16 * r, 1)
+        inner_out[pl.ds(r, DEVICES, stride=8), :] = jnp.where(lane_at < INNER, slots[r], tail)
 
     for face_id in range(4):
         pair = face_id // 2
@@ -345,19 +363,24 @@
     for copy in halos:
         copy.start()
 
-    def exchange(source, target, send_sem, recv_sem):
+    def block(ref, device, rows):
+        return ref.at[pl.ds(pl.multiple_of(device * 8, 8), rows)]
+
+    def exchange(source, target, rows, send_sem, recv_sem):
         for to in others:
             pltpu.make_async_remote_copy(
-                src_ref=source.at[to],
-                dst_ref=target.at[me],
+                src_ref=block(source, to, rows),
+                dst_ref=block(target, me, rows),
                 send_sem=send_sem,
                 recv_sem=recv_sem,
                 device_id=(to,),
                 device_id_type=MESH,
             ).start()
 
-    exchange(inner_out, inner_in, inner_send, inner_recv)
-    own_inner = pltpu.make_async_copy(inner_out.at[me], inner_in.at[me], own_sem.at[0])
+    exchange(inner_out, inner_in, INNER_ROWS, inner_send, inner_recv)
+    own_inner = pltpu.make_async_copy(
+        block(inner_out, me, INNER_ROWS), block(inner_in, me, INNER_ROWS), own_sem.at[0]
+    )
     own_inner.start()
 
     for copy in halos:
@@ -405,16 +428,28 @@
                     jump + largest * (outside[field] - inside[field])
                 )
     outer = [
-        stepped[field][INNER:] + jnp.concatenate(lifted[field], axis=0) for field in range(3)
+        stepped[field][MAIN : MAIN + OUTER] + jnp.concatenate(lifted[field], axis=0)
+        for field in range(3)
     ]
-    place(jnp.concatenate(outer + [jnp.zeros((32, ELEMS), f32)], axis=0), outer_out)
-
-    exchange(outer_out, outer_in, outer_send, outer_recv)
-    own_outer = pltpu.make_async_copy(outer_out.at[me], outer_in.at[me], own_sem.at[1])
+    slots = place(jnp.concatenate(outer + [jnp.zeros((LANES - 96, ELEMS), f32)], axis=0))
+    for r in range(4):
+        pair_of = jnp.where(lane_at < 64, slots[r], pltpu.roll(slots[r + 4], 64, 1))
+        outer_out[pl.ds(r, DEVICES, stride=8), :] = pair_of
+    for q in range(2):
+        row = pltpu.roll(slots[4 * q], 64, 1)
+        for k in range(1, 4):
+            piece = slots[4 * q + k] if k == 2 else pltpu.roll(slots[4 * q + k], (32 * k - 64) % 128, 1)
+            row = jnp.where(lane_at >= 32 * k, piece, row)
+        outer_out[pl.ds(4 + q, DEVICES, stride=8), :] = row
+
+    exchange(outer_out, outer_in, OUTER_ROWS, outer_send, outer_recv)
+    own_outer = pltpu.make_async_copy(
+        block(outer_out, me, OUTER_ROWS), block(outer_in, me, OUTER_ROWS), own_sem.at[1]
+    )
     own_outer.start()
 
-    def wait_all(source, target, send_sem, recv_sem):
-        every = pl.ds(0, DEVICES - 1)
+    def wait_all(source, target, rows, send_sem, recv_sem):
+        every = pl.ds(0, (DEVICES - 1) * rows)
         copies = pltpu.make_async_remote_copy(
             src_ref=source.at[every],
             dst_ref=target.at[every],
@@ -427,37 +462,77 @@
         copies.wait_recv()
 
     own_inner.wait()
+    wait_all(inner_out, inner_in, INNER_ROWS, inner_send, inner_recv)
+    last = None
+    for r in range(INNER_ROWS):
+        tail = pltpu.roll(inner_in[pl.ds(r, DEVICES, stride=8), :], 16 * r + 16, 1)
+        last = tail if r == 0 else jnp.where(lane_at >= 16 * r, tail, last)
+    inner_in[pl.ds(7, DEVICES, stride=8), :] = last
+    inner_turned[...] = jnp.transpose(inner_in[...])[:INNER]
+    turned = pltpu.make_async_copy(inner_turned, inner_turned_out, own_sem.at[2])
+    turned.start()
     own_outer.wait()
-    wait_all(inner_out, inner_in, inner_send, inner_recv)
-    wait_all(outer_out, outer_in, outer_send, outer_recv)
-
-
-def child_kernel(inner, outer, high_table, low_table, out):
-    columns = inner.shape[0]
-    inner_high, inner_low = split2(inner[...])
-    outer_high, outer_low = split2(outer[...])
-    high = jnp.concatenate([inner_high, outer_high], axis=1)
-    low = jnp.concatenate([inner_low, outer_low], axis=1)
-    dims = (((1,), (1,)), ((), ()))
-    main = lax.dot_general(
-        high_table[...], high, dims, preferred_element_type=f32
-    ) + lax.dot_general(high_table[...], low, dims, preferred_element_type=f32)
-    fine = lax.dot_general(low_table[...], high, dims, preferred_element_type=f32)
-    refined = jnp.broadcast_to(main[960:961] > 0.5, (192, columns))
-    out[0:192, :] = jnp.where(refined, main[0:192] + fine[0:192], main[768:960])
-    for c in range(1, 4):
-        rows = slice(192 * c, 192 * c + 192)
-        out[rows, :] = jnp.where(refined, main[rows] + fine[rows], 0.0)
+    turned.wait()
+    wait_all(outer_out, outer_in, OUTER_ROWS, outer_send, outer_recv)
+
+
+def child_kernel(inner_in, outer_in, tables_in, out_hbm, inner, outer, tables, flat, out, load_sem, store_sem):
+    loads = [
+        pltpu.make_async_copy(outer_in, outer, load_sem.at[0]),
+        pltpu.make_async_copy(inner_in, inner, load_sem.at[1]),
+        pltpu.make_async_copy(tables_in, tables, load_sem.at[2]),
+    ]
+    for load in loads:
+        load.start()
+    loads[0].wait()
+    lane_at = lax.broadcasted_iota(jnp.int32, (DEVICES, LANES), 1)
+    for j in range(SLOTS):
+        body = outer[pl.ds(j % 4, DEVICES, stride=8), :]
+        rest = outer[pl.ds(4 + j // 4, DEVICES, stride=8), :]
+        body = pltpu.roll(body, 64, 1) if j >= 4 else body
+        rest = rest if j % 4 == 2 else pltpu.roll(rest, (64 - 32 * (j % 4)) % 128, 1)
+        flat[pl.ds(j, DEVICES, stride=8), :] = jnp.where(lane_at < 64, body, rest)
+    faces = jnp.transpose(flat[...])
+    loads[1].wait()
+    loads[2].wait()
+    slots = DEVICES * SLOTS
+    refined = inner[3 * MAIN + FLAG : 3 * MAIN + FLAG + 1, :] > 0.5
+    stores = []
+    for field in range(3):
+        own = slice(MAIN * field, MAIN * field + MAIN)
+        start = 3 * MAIN + 8 * (field // 2)
+        values = jnp.concatenate(
+            [inner[own, :], faces[own], inner[start : start + 8, :], jnp.zeros((8, slots), f32)],
+            axis=0,
+        )
+        high, low = split2(values)
+        operand = jnp.concatenate([high, low, high, jnp.zeros((16, slots), bf16)], axis=0)
+        nodes = jnp.dot(tables[field % 2], operand, preferred_element_type=f32)
+        for c in range(4):
+            start = 192 * c + 64 * field
+            rows = pl.ds(start, 64)
+            other = nodes[256:320] if c == 0 else 0.0
+            out[start : start + 64, :] = jnp.where(refined, nodes[64 * c : 64 * c + 64], other)
+            store = pltpu.make_async_copy(
+                out.at[rows], out_hbm.at[rows], store_sem.at[4 * field + c]
+            )
+            store.start()
+            stores.append(store)
+    for store in stores:
+        store.wait()
 
 
 def on_device(state, neighbours, metric, flags, new_owner):
     hbm = pl.BlockSpec(memory_space=pl.ANY)
-    block = jax.ShapeDtypeStruct((DEVICES, SLOTS, LANES), f32)
-    buffer = pltpu.VMEM((DEVICES, SLOTS, LANES), f32)
+    slots = DEVICES * SLOTS
+    buffer = pltpu.VMEM((slots, LANES), f32)
     dma = pltpu.SemaphoreType.DMA
     inner, outer = pl.pallas_call(
         step_kernel,
-        out_shape=(block, block),
+        out_shape=(
+            jax.ShapeDtypeStruct((INNER, slots), f32),
+            jax.ShapeDtypeStruct((slots, LANES), f32),
+        ),
         in_specs=[hbm] * 6,
         out_specs=(hbm, hbm),
         scratch_shapes=[
@@ -466,7 +541,7 @@
             pltpu.VMEM((1, ELEMS), f32),
             pltpu.VMEM((1, ELEMS), jnp.int32),
             pltpu.VMEM((1, ELEMS), jnp.int32),
-            pltpu.VMEM((INNER + OUTER, 512), bf16),
+            pltpu.VMEM((240, 512), bf16),
             pltpu.VMEM((192 * ELEMS // LANES, LANES), f32),
             pltpu.VMEM((2, 48, ELEMS), f32),
             pltpu.VMEM((4, 32, ELEMS), f32),
@@ -475,7 +550,10 @@
             pltpu.VMEM((2, 2, 32, LANES), f32),
             buffer,
             buffer,
-            pltpu.VMEM((DEVICES * SLOTS, ELEMS), bf16),
+            buffer,
+            buffer,
+            pltpu.VMEM((INNER, slots), f32),
+            pltpu.VMEM((slots, ELEMS), bf16),
             dma((6,)),
             dma((2, 2)),
             dma((2, 2)),
@@ -483,7 +561,7 @@
             dma,
             dma,
             dma,
-            dma((2,)),
+            dma((3,)),
         ],
         compiler_params=pltpu.CompilerParams(collective_id=0, has_side_effects=True),
         name="step_and_migrate",
@@ -495,27 +573,22 @@
         new_owner.reshape(1, ELEMS),
         jnp.asarray(step_table(), bf16),
     )
-    slots = DEVICES * SLOTS
-    tile = 256
-    high_table, low_table = child_table()
     children = pl.pallas_call(
         child_kernel,
-        grid=(slots // tile,),
         out_shape=jax.ShapeDtypeStruct((768, slots), f32),
-        in_specs=[
-            pl.BlockSpec((tile, LANES), lambda i: (i, 0)),
-            pl.BlockSpec((tile, LANES), lambda i: (i, 0)),
-            pl.BlockSpec((968, 2 * LANES), lambda i: (0, 0)),
-            pl.BlockSpec((768, 2 * LANES), lambda i: (0, 0)),
+        in_specs=[hbm] * 3,
+        out_specs=hbm,
+        scratch_shapes=[
+            pltpu.VMEM((INNER, slots), f32),
+            buffer,
+            pltpu.VMEM((2, 320, 256), bf16),
+            buffer,
+            pltpu.VMEM((768, slots), f32),
+            dma((3,)),
+            dma((12,)),
         ],
-        out_specs=pl.BlockSpec((768, tile), lambda i: (0, i)),
         name="make_children",
-    )(
-        inner.reshape(slots, LANES),
-        outer.reshape(slots, LANES),
-        jnp.asarray(high_table, bf16),
-        jnp.asarray(low_table, bf16),
-    )
+    )(inner, outer, jnp.asarray(child_tables(), bf16))
     return children.reshape(4, 3, 64, slots)
 
 

time: 33 us -> 26.8 us (0.81)
  Pallas kernels: 32.8 us -> 26.7 us
    pallas_call x2, Pallas kernels: 32.8 us -> 26.7 us  [the longest x1 23.1 us: on_device(): pl.pallas_call(step_kernel, out_shape=(jax.ShapeDtypeStruct((INNER, slots...]
where the time goes in v3:
time: 26.8 us; the launch traced here: 26.7 us
  Pallas kernels  26.7 us (100%)
    pallas_call x1, Pallas kernels, on_device(): pl.pallas_call(step_kernel, out_shape=(jax.ShapeDtypeStruct((INNER, slots...  23.1 us
    pallas_call x1, Pallas kernels, on_device(): pl.pallas_call(child_kernel, out_shape=jax.ShapeDtypeStruct((768, slots),...  3.59 us

profile of v3, /device:TPU:1, one launch (start us, length us, event | category | flops | bytes accessed | tf_op | source)
XLA Modules:
  0.0 26.7 jit_solution(352692244243316512)
XLA Ops:
  0.0 23.1 %step_and_migrate.1 = (f32[112,1024]{1,0:T(8,128)}, f32[1024,128]{1,0:T(8,128)}) custom-call(f32[192,512]{1,0:T(8,128)} %bitcast.5, s32[4,512]{1,0:T(4,128)} %neighbours_in.1, f32[1,512]{1,0:T(1,128)} %bitcast.6, s32[1,512]{1,0:T(1,128)} %bitcast.7, s32[1,512]{1,0:T(1,128)} %bitcast.8, bf16[240,512]{1,0:T(8,128)(2,1)} %constant.4.clone.table_in), custom_call_target="tpu_custom_call" | custom-call | tf_op jit(solution)/shard_map/step_and_migrate/pallas_call | solution.py:530
  23.1 3.6 %make_children.1 = f32[768,1024]{1,0:T(8,128)} custom-call(f32[112,1024]{1,0:T(8,128)} %get-tuple-element.7.inner_in, f32[1024,128]{1,0:T(8,128)} %get-tuple-element.8.outer_in, bf16[2,320,256]{2,1,0:T(8,128)(2,1)} %constant.5.clone.tables_in), custom_call_target="tpu_custom_call" | custom-call | tf_op jit(solution)/shard_map/make_children/pallas_call | solution.py:576

commit v4 on v3

--- a/solution.py
+++ b/solution.py
@@ -169,8 +169,8 @@
 
 
 def step_kernel(
-    state_in, neighbours_in, metric_in, flags_in, owner_in, table_in,
-    inner_turned_out, outer_in,
+    state_in, neighbours_in, metric_in, flags_in, owner_in, table_in, tables_in,
+    inner_turned_out, outer_in, tables_out,
     state, neighbours, metric, flags, owner, table,
     tiles, trace, own_flux, across, crossing, ghost,
     placed, inner_out, outer_out, inner_in, inner_turned, onehot,
@@ -461,6 +461,8 @@
         copies.wait_send()
         copies.wait_recv()
 
+    tables_load = pltpu.make_async_copy(tables_in, tables_out, own_sem.at[3])
+    tables_load.start()
     own_inner.wait()
     wait_all(inner_out, inner_in, INNER_ROWS, inner_send, inner_recv)
     last = None
@@ -473,18 +475,11 @@
     turned.start()
     own_outer.wait()
     turned.wait()
+    tables_load.wait()
     wait_all(outer_out, outer_in, OUTER_ROWS, outer_send, outer_recv)
 
 
-def child_kernel(inner_in, outer_in, tables_in, out_hbm, inner, outer, tables, flat, out, load_sem, store_sem):
-    loads = [
-        pltpu.make_async_copy(outer_in, outer, load_sem.at[0]),
-        pltpu.make_async_copy(inner_in, inner, load_sem.at[1]),
-        pltpu.make_async_copy(tables_in, tables, load_sem.at[2]),
-    ]
-    for load in loads:
-        load.start()
-    loads[0].wait()
+def child_kernel(inner, outer, tables, out_hbm, flat, out, store_sem):
     lane_at = lax.broadcasted_iota(jnp.int32, (DEVICES, LANES), 1)
     for j in range(SLOTS):
         body = outer[pl.ds(j % 4, DEVICES, stride=8), :]
@@ -493,8 +488,6 @@
         rest = rest if j % 4 == 2 else pltpu.roll(rest, (64 - 32 * (j % 4)) % 128, 1)
         flat[pl.ds(j, DEVICES, stride=8), :] = jnp.where(lane_at < 64, body, rest)
     faces = jnp.transpose(flat[...])
-    loads[1].wait()
-    loads[2].wait()
     slots = DEVICES * SLOTS
     refined = inner[3 * MAIN + FLAG : 3 * MAIN + FLAG + 1, :] > 0.5
     stores = []
@@ -527,14 +520,15 @@
     slots = DEVICES * SLOTS
     buffer = pltpu.VMEM((slots, LANES), f32)
     dma = pltpu.SemaphoreType.DMA
-    inner, outer = pl.pallas_call(
+    inner, outer, tables = pl.pallas_call(
         step_kernel,
         out_shape=(
             jax.ShapeDtypeStruct((INNER, slots), f32),
             jax.ShapeDtypeStruct((slots, LANES), f32),
+            jax.ShapeDtypeStruct((2, 320, 256), bf16),
         ),
-        in_specs=[hbm] * 6,
-        out_specs=(hbm, hbm),
+        in_specs=[pl.BlockSpec(memory_space=pltpu.HBM)] * 7,
+        out_specs=(hbm, hbm, hbm),
         scratch_shapes=[
             pltpu.VMEM((192, ELEMS), f32),
             pltpu.VMEM((4, ELEMS), jnp.int32),
@@ -561,34 +555,37 @@
             dma,
             dma,
             dma,
-            dma((3,)),
+            dma((4,)),
         ],
-        compiler_params=pltpu.CompilerParams(collective_id=0, has_side_effects=True),
+        compiler_params=pltpu.CompilerParams(collective_id=0, has_side_effects=True, vmem_limit_bytes=16 << 20),
         name="step_and_migrate",
     )(
-        state.reshape(192, ELEMS),
-        neighbours,
-        metric.reshape(1, ELEMS),
-        flags.reshape(1, ELEMS),
-        new_owner.reshape(1, ELEMS),
-        jnp.asarray(step_table(), bf16),
+        *(
+            pltpu.with_memory_space_constraint(x, pltpu.HBM)
+            for x in (
+                state.reshape(192, ELEMS),
+                neighbours,
+                metric.reshape(1, ELEMS),
+                flags.reshape(1, ELEMS),
+                new_owner.reshape(1, ELEMS),
+                jnp.asarray(step_table(), bf16),
+                jnp.asarray(child_tables(), bf16),
+            )
+        )
     )
     children = pl.pallas_call(
         child_kernel,
         out_shape=jax.ShapeDtypeStruct((768, slots), f32),
-        in_specs=[hbm] * 3,
-        out_specs=hbm,
+        in_specs=[pl.BlockSpec(memory_space=pltpu.VMEM)] * 3,
+        out_specs=pl.BlockSpec(memory_space=pltpu.HBM),
         scratch_shapes=[
-            pltpu.VMEM((INNER, slots), f32),
-            buffer,
-            pltpu.VMEM((2, 320, 256), bf16),
             buffer,
             pltpu.VMEM((768, slots), f32),
-            dma((3,)),
             dma((12,)),
         ],
+        compiler_params=pltpu.CompilerParams(vmem_limit_bytes=16 << 20),
         name="make_children",
-    )(inner, outer, jnp.asarray(child_tables(), bf16))
+    )(inner, outer, tables)
     return children.reshape(4, 3, 64, slots)
 
 

time: 26.8 us -> 27.4 us (1.022)
  Pallas kernels: 26.7 us -> 27.3 us
    pallas_call x1, Pallas kernels: 23.1 us -> 24.8 us  [on_device(): pl.pallas_call(step_kernel, out_shape=(jax.ShapeDtypeStruct((INNER, slots...]
    pallas_call x1, Pallas kernels: 3.59 us -> 2.47 us  [on_device(): pl.pallas_call(child_kernel, out_shape=jax.ShapeDtypeStruct((768, slots),...]
where the time goes in v4:
time: 27.4 us; the launch traced here: 27.3 us
  Pallas kernels  27.3 us (100%)
    pallas_call x1, Pallas kernels, on_device(): pl.pallas_call(step_kernel, out_shape=(jax.ShapeDtypeStruct((INNER, slots...  24.8 us
    pallas_call x1, Pallas kernels, on_device(): pl.pallas_call(child_kernel, out_shape=jax.ShapeDtypeStruct((768, slots),...  2.47 us

profile of v4, /device:TPU:1, one launch (start us, length us, event | category | flops | bytes accessed | tf_op | source)
XLA Modules:
  0.0 27.3 jit_solution(14579143745418332556)
XLA Ops:
  0.0 24.8 %step_and_migrate.1 = (f32[112,1024]{1,0:T(8,128)S(1)}, f32[1024,128]{1,0:T(8,128)S(1)}, bf16[2,320,256]{2,1,0:T(8,128)(2,1)S(1)}) custom-call(f32[192,512]{1,0:T(8,128)} %bitcast.5, s32[4,512]{1,0:T(4,128)} %neighbours_in.1, f32[1,512]{1,0:T(1,128)} %bitcast.6, s32[1,512]{1,0:T(1,128)} %bitcast.7, s32[1,512]{1,0:T(1,128)} %bitcast.8, ...), custom_call_target="tpu_custom_call" | custom-call | tf_op jit(solution)/shard_map/step_and_migrate/pallas_call | solution.py:523
  24.8 2.5 %make_children.1 = f32[768,1024]{1,0:T(8,128)} custom-call(f32[112,1024]{1,0:T(8,128)S(1)} %get-tuple-element.8.inner, f32[1024,128]{1,0:T(8,128)S(1)} %get-tuple-element.9.outer, bf16[2,320,256]{2,1,0:T(8,128)(2,1)S(1)} %get-tuple-element.10.tables), custom_call_target="tpu_custom_call" | custom-call | tf_op jit(solution)/shard_map/make_children/pallas_call | solution.py:576

commit v5 on v4

--- a/solution.py
+++ b/solution.py
@@ -134,12 +134,13 @@
     return np.stack(tables)
 
 
-def send_order():
+def distances(seed, far_first):
     order = [
         (z, y, x, c) for z in range(4) for y in range(4) for x in range(4) for c in range(2)
     ][1:]
-    random.Random(0).shuffle(order)
-    order.sort(key=lambda d: -sum(min(v, 4 - v) for v in d[:3]))
+    random.Random(seed).shuffle(order)
+    if far_first:
+        order.sort(key=lambda d: -sum(min(v, 4 - v) for v in d[:3]))
     return order
 
 
@@ -185,17 +186,18 @@
         load.start()
 
     me = lax.axis_index("curve")
-    order = send_order()
     z_part = [lax.rem(me // 32 + z, 4) * 32 for z in range(4)]
     y_part = [lax.rem((me // 8) % 4 + y, 4) * 8 for y in range(4)]
     x_part = [lax.rem((me // 2) % 4 + x, 4) * 2 for x in range(4)]
     c_part = [lax.rem(me % 2 + c, 2) for c in range(2)]
     zy_part = [[z + y for y in y_part] for z in z_part]
     xc_part = [[x + c for c in c_part] for x in x_part]
-    others = [zy_part[z][y] + xc_part[x][c] for z, y, x, c in order]
+
+    def others(seed, far_first):
+        return [zy_part[z][y] + xc_part[x][c] for z, y, x, c in distances(seed, far_first)]
 
     barrier = pltpu.get_barrier_semaphore()
-    for to in others:
+    for to in others(0, True):
         pl.semaphore_signal(barrier, inc=1, device_id=(to,), device_id_type=MESH)
     for load in loads:
         load.wait()
@@ -366,8 +368,8 @@
     def block(ref, device, rows):
         return ref.at[pl.ds(pl.multiple_of(device * 8, 8), rows)]
 
-    def exchange(source, target, rows, send_sem, recv_sem):
-        for to in others:
+    def exchange(order, source, target, rows, send_sem, recv_sem):
+        for to in order:
             pltpu.make_async_remote_copy(
                 src_ref=block(source, to, rows),
                 dst_ref=block(target, me, rows),
@@ -377,7 +379,7 @@
                 device_id_type=MESH,
             ).start()
 
-    exchange(inner_out, inner_in, INNER_ROWS, inner_send, inner_recv)
+    exchange(others(2, False), inner_out, inner_in, INNER_ROWS, inner_send, inner_recv)
     own_inner = pltpu.make_async_copy(
         block(inner_out, me, INNER_ROWS), block(inner_in, me, INNER_ROWS), own_sem.at[0]
     )
@@ -442,7 +444,7 @@
             row = jnp.where(lane_at >= 32 * k, piece, row)
         outer_out[pl.ds(4 + q, DEVICES, stride=8), :] = row
 
-    exchange(outer_out, outer_in, OUTER_ROWS, outer_send, outer_recv)
+    exchange(others(1, True), outer_out, outer_in, OUTER_ROWS, outer_send, outer_recv)
     own_outer = pltpu.make_async_copy(
         block(outer_out, me, OUTER_ROWS), block(outer_in, me, OUTER_ROWS), own_sem.at[1]
     )

time: 27.4 us -> 25.2 us (0.920)
  Pallas kernels: 27.3 us -> 25 us
    pallas_call x1, Pallas kernels: 24.8 us -> 22.6 us  [on_device(): pl.pallas_call(step_kernel, out_shape=(jax.ShapeDtypeStruct((INNER, slots...]
where the time goes in v5:
time: 25.2 us; the launch traced here: 25 us
  Pallas kernels  25 us (99%)
    pallas_call x1, Pallas kernels, on_device(): pl.pallas_call(step_kernel, out_shape=(jax.ShapeDtypeStruct((INNER, slots...  22.6 us
    pallas_call x1, Pallas kernels, on_device(): pl.pallas_call(child_kernel, out_shape=jax.ShapeDtypeStruct((768, slots),...  2.47 us

profile of v5, /device:TPU:1, one launch (start us, length us, event | category | flops | bytes accessed | tf_op | source)
XLA Modules:
  0.0 25.0 jit_solution(8000642833220476471)
XLA Ops:
  0.0 22.6 %step_and_migrate.1 = (f32[112,1024]{1,0:T(8,128)S(1)}, f32[1024,128]{1,0:T(8,128)S(1)}, bf16[2,320,256]{2,1,0:T(8,128)(2,1)S(1)}) custom-call(f32[192,512]{1,0:T(8,128)} %bitcast.5, s32[4,512]{1,0:T(4,128)} %neighbours_in.1, f32[1,512]{1,0:T(1,128)} %bitcast.6, s32[1,512]{1,0:T(1,128)} %bitcast.7, s32[1,512]{1,0:T(1,128)} %bitcast.8, ...), custom_call_target="tpu_custom_call" | custom-call | tf_op jit(solution)/shard_map/step_and_migrate/pallas_call | solution.py:525
  22.6 2.5 %make_children.1 = f32[768,1024]{1,0:T(8,128)} custom-call(f32[112,1024]{1,0:T(8,128)S(1)} %get-tuple-element.8.inner, f32[1024,128]{1,0:T(8,128)S(1)} %get-tuple-element.9.outer, bf16[2,320,256]{2,1,0:T(8,128)(2,1)S(1)} %get-tuple-element.10.tables), custom_call_target="tpu_custom_call" | custom-call | tf_op jit(solution)/shard_map/make_children/pallas_call | solution.py:578

commit v6 on v5

--- a/solution.py
+++ b/solution.py
@@ -174,7 +174,7 @@
     inner_turned_out, outer_in, tables_out,
     state, neighbours, metric, flags, owner, table,
     tiles, trace, own_flux, across, crossing, ghost,
-    placed, inner_out, outer_out, inner_in, inner_turned, onehot,
+    inner_out, outer_out, inner_in, inner_turned, onehot,
     load_sem, halo_send, halo_recv, inner_send, inner_recv, outer_send, outer_recv, own_sem,
 ):
     pairs = (
@@ -211,17 +211,21 @@
     owners = owner[...]
     hits = owners == lax.broadcasted_iota(jnp.int32, (DEVICES, ELEMS), 0)
     hits = jnp.where(hits, 1.0, 0.0)
-    earlier = lax.broadcasted_iota(jnp.int32, (ELEMS, ELEMS), 0) < lax.broadcasted_iota(
-        jnp.int32, (ELEMS, ELEMS), 1
-    )
     nothing = jnp.zeros((4, ELEMS), f32)
-    before = jnp.dot(
-        jnp.concatenate([hits, below, nothing, above, nothing], axis=0).astype(bf16),
-        jnp.where(earlier, 1.0, 0.0).astype(bf16),
-        preferred_element_type=f32,
-    )
+    marks = jnp.concatenate([hits, below, nothing, above, nothing], axis=0).astype(bf16)
+    at_row = lax.broadcasted_iota(jnp.int32, (LANES, 2 * LANES), 0)
+    at_lane = lax.broadcasted_iota(jnp.int32, (LANES, 2 * LANES), 1)
+    earlier = jnp.where((at_row < at_lane) | (at_lane >= LANES), 1.0, 0.0).astype(bf16)
+    before, total = [], None
+    for t in range(ELEMS // LANES):
+        count = jnp.dot(
+            marks[:, LANES * t : LANES * t + LANES], earlier, preferred_element_type=f32
+        )
+        before.append(count[:, :LANES] if t == 0 else count[:, :LANES] + total)
+        total = count[:, LANES:] if t == 0 else count[:, LANES:] + total
+    before = jnp.concatenate(before, axis=1)
     rank = jnp.sum(hits * before[:DEVICES], axis=0, keepdims=True)
-    column = owners * SLOTS + rank.astype(jnp.int32)
+    column = rank.astype(jnp.int32) * DEVICES + owners
     slot_rows = lax.broadcasted_iota(jnp.int32, (DEVICES * SLOTS, ELEMS), 0)
     onehot[...] = jnp.where(slot_rows == column, 1.0, 0.0).astype(bf16)
     spot = jnp.where(
@@ -305,8 +309,8 @@
             nt_dims,
             preferred_element_type=f32,
         )
-        placed[...] = both[:, :LANES] + both[:, LANES:]
-        return [placed[pl.ds(j, DEVICES, stride=SLOTS), :] for j in range(SLOTS)]
+        both = both[:, :LANES] + both[:, LANES:]
+        return [both[j * DEVICES : (j + 1) * DEVICES] for j in range(SLOTS)]
 
     lane_at = lax.broadcasted_iota(jnp.int32, (DEVICES, LANES), 1)
     extra = stepped[0][-EXTRA:] + stepped[1][-EXTRA:] + stepped[2][-EXTRA:]
@@ -320,6 +324,45 @@
     for r in range(INNER_ROWS):
         tail = pltpu.roll(slots[7], INNER - 16 * r, 1)
         inner_out[pl.ds(r, DEVICES, stride=8), :] = jnp.where(lane_at < INNER, slots[r], tail)
+
+    pl.semaphore_wait(barrier, DEVICES - 1)
+
+    def halo(pair, upward):
+        far = 32 if pair else 1
+        target = lax.rem(me + (far if upward else DEVICES - far), DEVICES)
+        side = 0 if upward else 1
+        return pltpu.make_async_remote_copy(
+            src_ref=crossing.at[pair],
+            dst_ref=ghost.at[pair, side],
+            send_sem=halo_send.at[pair, side],
+            recv_sem=halo_recv.at[pair, side],
+            device_id=(target,),
+            device_id_type=MESH,
+        )
+
+    halos = [halo(pair, upward) for pair in (0, 1) for upward in (True, False)]
+    for copy in halos:
+        copy.start()
+
+    def block(ref, device, rows):
+        return ref.at[pl.ds(pl.multiple_of(device * 8, 8), rows)]
+
+    def exchange(order, source, target, rows, send_sem, recv_sem):
+        for to in order:
+            pltpu.make_async_remote_copy(
+                src_ref=block(source, to, rows),
+                dst_ref=block(target, me, rows),
+                send_sem=send_sem,
+                recv_sem=recv_sem,
+                device_id=(to,),
+                device_id_type=MESH,
+            ).start()
+
+    exchange(others(2, False), inner_out, inner_in, INNER_ROWS, inner_send, inner_recv)
+    own_inner = pltpu.make_async_copy(
+        block(inner_out, me, INNER_ROWS), block(inner_in, me, INNER_ROWS), own_sem.at[0]
+    )
+    own_inner.start()
 
     for face_id in range(4):
         pair = face_id // 2
@@ -345,45 +388,6 @@
                     got = jnp.take_along_axis(values, index, axis=1, mode="promise_in_bounds")
                     found = got if c == 0 else jnp.where(piece_t == c, got, found)
                 across[face_id, 8 * field : 8 * field + 8, cols] = found
-
-    pl.semaphore_wait(barrier, DEVICES - 1)
-
-    def halo(pair, upward):
-        far = 32 if pair else 1
-        target = lax.rem(me + (far if upward else DEVICES - far), DEVICES)
-        side = 0 if upward else 1
-        return pltpu.make_async_remote_copy(
-            src_ref=crossing.at[pair],
-            dst_ref=ghost.at[pair, side],
-            send_sem=halo_send.at[pair, side],
-            recv_sem=halo_recv.at[pair, side],
-            device_id=(target,),
-            device_id_type=MESH,
-        )
-
-    halos = [halo(pair, upward) for pair in (0, 1) for upward in (True, False)]
-    for copy in halos:
-        copy.start()
-
-    def block(ref, device, rows):
-        return ref.at[pl.ds(pl.multiple_of(device * 8, 8), rows)]
-
-    def exchange(order, source, target, rows, send_sem, recv_sem):
-        for to in order:
-            pltpu.make_async_remote_copy(
-                src_ref=block(source, to, rows),
-                dst_ref=block(target, me, rows),
-                send_sem=send_sem,
-                recv_sem=recv_sem,
-                device_id=(to,),
-                device_id_type=MESH,
-            ).start()
-
-    exchange(others(2, False), inner_out, inner_in, INNER_ROWS, inner_send, inner_recv)
-    own_inner = pltpu.make_async_copy(
-        block(inner_out, me, INNER_ROWS), block(inner_in, me, INNER_ROWS), own_sem.at[0]
-    )
-    own_inner.start()
 
     for copy in halos:
         copy.wait()
@@ -482,37 +486,55 @@
 
 
 def child_kernel(inner, outer, tables, out_hbm, flat, out, store_sem):
-    lane_at = lax.broadcasted_iota(jnp.int32, (DEVICES, LANES), 1)
-    for j in range(SLOTS):
-        body = outer[pl.ds(j % 4, DEVICES, stride=8), :]
-        rest = outer[pl.ds(4 + j // 4, DEVICES, stride=8), :]
-        body = pltpu.roll(body, 64, 1) if j >= 4 else body
-        rest = rest if j % 4 == 2 else pltpu.roll(rest, (64 - 32 * (j % 4)) % 128, 1)
-        flat[pl.ds(j, DEVICES, stride=8), :] = jnp.where(lane_at < 64, body, rest)
-    faces = jnp.transpose(flat[...])
-    slots = DEVICES * SLOTS
-    refined = inner[3 * MAIN + FLAG : 3 * MAIN + FLAG + 1, :] > 0.5
+    parts = 2
+    devices, slots = DEVICES // parts, DEVICES * SLOTS // parts
+    lane_at = lax.broadcasted_iota(jnp.int32, (devices, LANES), 1)
+
+    def unpack(part):
+        first = part * slots
+        for j in range(SLOTS):
+            body = outer[pl.ds(first + j % 4, devices, stride=8), :]
+            rest = outer[pl.ds(first + 4 + j // 4, devices, stride=8), :]
+            body = pltpu.roll(body, 64, 1) if j >= 4 else body
+            rest = rest if j % 4 == 2 else pltpu.roll(rest, (64 - 32 * (j % 4)) % 128, 1)
+            flat[pl.ds(first + j, devices, stride=8), :] = jnp.where(lane_at < 64, body, rest)
+        return jnp.transpose(flat[first : first + slots, :])
+
     stores = []
-    for field in range(3):
-        own = slice(MAIN * field, MAIN * field + MAIN)
-        start = 3 * MAIN + 8 * (field // 2)
-        values = jnp.concatenate(
-            [inner[own, :], faces[own], inner[start : start + 8, :], jnp.zeros((8, slots), f32)],
-            axis=0,
-        )
-        high, low = split2(values)
-        operand = jnp.concatenate([high, low, high, jnp.zeros((16, slots), bf16)], axis=0)
-        nodes = jnp.dot(tables[field % 2], operand, preferred_element_type=f32)
-        for c in range(4):
-            start = 192 * c + 64 * field
-            rows = pl.ds(start, 64)
-            other = nodes[256:320] if c == 0 else 0.0
-            out[start : start + 64, :] = jnp.where(refined, nodes[64 * c : 64 * c + 64], other)
-            store = pltpu.make_async_copy(
-                out.at[rows], out_hbm.at[rows], store_sem.at[4 * field + c]
+    ahead = unpack(0)
+    for part in range(parts):
+        columns = slice(part * slots, part * slots + slots)
+        faces = ahead
+        refined = inner[3 * MAIN + FLAG : 3 * MAIN + FLAG + 1, columns] > 0.5
+        for field in range(3):
+            own = slice(MAIN * field, MAIN * field + MAIN)
+            start = 3 * MAIN + 8 * (field // 2)
+            values = jnp.concatenate(
+                [
+                    inner[own, columns],
+                    faces[own],
+                    inner[start : start + 8, columns],
+                    jnp.zeros((8, slots), f32),
+                ],
+                axis=0,
             )
-            store.start()
-            stores.append(store)
+            high, low = split2(values)
+            operand = jnp.concatenate([high, low, high, jnp.zeros((16, slots), bf16)], axis=0)
+            nodes = jnp.dot(tables[field % 2], operand, preferred_element_type=f32)
+            if field == 0 and part + 1 < parts:
+                ahead = unpack(part + 1)
+            for c in range(4):
+                start = 192 * c + 64 * field
+                other = nodes[256:320] if c == 0 else 0.0
+                out[start : start + 64, columns] = jnp.where(
+                    refined, nodes[64 * c : 64 * c + 64], other
+                )
+                box = (pl.ds(start, 64), pl.ds(part * slots, slots))
+                store = pltpu.make_async_copy(
+                    out.at[box], out_hbm.at[box], store_sem.at[12 * part + 4 * field + c]
+                )
+                store.start()
+                stores.append(store)
     for store in stores:
         store.wait()
 
@@ -547,7 +569,6 @@
             buffer,
             buffer,
             buffer,
-            buffer,
             pltpu.VMEM((INNER, slots), f32),
             pltpu.VMEM((slots, ELEMS), bf16),
             dma((6,)),
@@ -583,7 +604,7 @@
         scratch_shapes=[
             buffer,
             pltpu.VMEM((768, slots), f32),
-            dma((12,)),
+            dma((24,)),
         ],
         compiler_params=pltpu.CompilerParams(vmem_limit_bytes=16 << 20),
         name="make_children",

time: 25.2 us -> 25 us (level)
  no operation moved by 1% of the time
where the time goes in v6:
time: 25 us; the launch traced here: 24.9 us
  Pallas kernels  24.9 us (100%)
    pallas_call x1, Pallas kernels, on_device(): pl.pallas_call(step_kernel, out_shape=(jax.ShapeDtypeStruct((INNER, slots...  22.5 us
    pallas_call x1, Pallas kernels, on_device(): pl.pallas_call(child_kernel, out_shape=jax.ShapeDtypeStruct((768, slots),...  2.35 us

profile of v6, /device:TPU:1, one launch (start us, length us, event | category | flops | bytes accessed | tf_op | source)
XLA Modules:
  0.0 24.9 jit_solution(7132755974352038328)
XLA Ops:
  0.0 22.5 %step_and_migrate.1 = (f32[112,1024]{1,0:T(8,128)S(1)}, f32[1024,128]{1,0:T(8,128)S(1)}, bf16[2,320,256]{2,1,0:T(8,128)(2,1)S(1)}) custom-call(f32[192,512]{1,0:T(8,128)} %bitcast.5, s32[4,512]{1,0:T(4,128)} %neighbours_in.1, f32[1,512]{1,0:T(1,128)} %bitcast.6, s32[1,512]{1,0:T(1,128)} %bitcast.7, s32[1,512]{1,0:T(1,128)} %bitcast.8, ...), custom_call_target="tpu_custom_call" | custom-call | tf_op jit(solution)/shard_map/step_and_migrate/pallas_call | solution.py:547
  22.5 2.4 %make_children.1 = f32[768,1024]{1,0:T(8,128)} custom-call(f32[112,1024]{1,0:T(8,128)S(1)} %get-tuple-element.8.inner, f32[1024,128]{1,0:T(8,128)S(1)} %get-tuple-element.9.outer, bf16[2,320,256]{2,1,0:T(8,128)(2,1)S(1)} %get-tuple-element.10.tables), custom_call_target="tpu_custom_call" | custom-call | tf_op jit(solution)/shard_map/make_children/pallas_call | solution.py:599

commit v7 on v6

--- a/solution.py
+++ b/solution.py
@@ -486,12 +486,12 @@
 
 
 def child_kernel(inner, outer, tables, out_hbm, flat, out, store_sem):
-    parts = 2
-    devices, slots = DEVICES // parts, DEVICES * SLOTS // parts
-    lane_at = lax.broadcasted_iota(jnp.int32, (devices, LANES), 1)
+    cuts = (0, 256, DEVICES * SLOTS)
 
     def unpack(part):
-        first = part * slots
+        first, slots = cuts[part], cuts[part + 1] - cuts[part]
+        devices = slots // SLOTS
+        lane_at = lax.broadcasted_iota(jnp.int32, (devices, LANES), 1)
         for j in range(SLOTS):
             body = outer[pl.ds(first + j % 4, devices, stride=8), :]
             rest = outer[pl.ds(first + 4 + j // 4, devices, stride=8), :]
@@ -502,8 +502,9 @@
 
     stores = []
     ahead = unpack(0)
-    for part in range(parts):
-        columns = slice(part * slots, part * slots + slots)
+    for part in range(2):
+        slots = cuts[part + 1] - cuts[part]
+        columns = slice(cuts[part], cuts[part + 1])
         faces = ahead
         refined = inner[3 * MAIN + FLAG : 3 * MAIN + FLAG + 1, columns] > 0.5
         for field in range(3):
@@ -521,7 +522,7 @@
             high, low = split2(values)
             operand = jnp.concatenate([high, low, high, jnp.zeros((16, slots), bf16)], axis=0)
             nodes = jnp.dot(tables[field % 2], operand, preferred_element_type=f32)
-            if field == 0 and part + 1 < parts:
+            if field == 0 and part == 0:
                 ahead = unpack(part + 1)
             for c in range(4):
                 start = 192 * c + 64 * field
@@ -529,7 +530,7 @@
                 out[start : start + 64, columns] = jnp.where(
                     refined, nodes[64 * c : 64 * c + 64], other
                 )
-                box = (pl.ds(start, 64), pl.ds(part * slots, slots))
+                box = (pl.ds(start, 64), pl.ds(cuts[part], slots))
                 store = pltpu.make_async_copy(
                     out.at[box], out_hbm.at[box], store_sem.at[12 * part + 4 * field + c]
                 )

time: 25 us -> 25 us (level)
  no operation moved by 1% of the time
where the time goes in v7:
time: 25 us; the launch traced here: 24.9 us
  Pallas kernels  24.9 us (100%)
    pallas_call x1, Pallas kernels, on_device(): pl.pallas_call(step_kernel, out_shape=(jax.ShapeDtypeStruct((INNER, slots...  22.5 us
    pallas_call x1, Pallas kernels, on_device(): pl.pallas_call(child_kernel, out_shape=jax.ShapeDtypeStruct((768, slots),...  2.4 us

profile of v7, /device:TPU:1, one launch (start us, length us, event | category | flops | bytes accessed | tf_op | source)
XLA Modules:
  0.0 24.9 jit_solution(7358629512484141457)
XLA Ops:
  0.0 22.5 %step_and_migrate.1 = (f32[112,1024]{1,0:T(8,128)S(1)}, f32[1024,128]{1,0:T(8,128)S(1)}, bf16[2,320,256]{2,1,0:T(8,128)(2,1)S(1)}) custom-call(f32[192,512]{1,0:T(8,128)} %bitcast.5, s32[4,512]{1,0:T(4,128)} %neighbours_in.1, f32[1,512]{1,0:T(1,128)} %bitcast.6, s32[1,512]{1,0:T(1,128)} %bitcast.7, s32[1,512]{1,0:T(1,128)} %bitcast.8, ...), custom_call_target="tpu_custom_call" | custom-call | tf_op jit(solution)/shard_map/step_and_migrate/pallas_call | solution.py:548
  22.5 2.4 %make_children.1 = f32[768,1024]{1,0:T(8,128)} custom-call(f32[112,1024]{1,0:T(8,128)S(1)} %get-tuple-element.8.inner, f32[1024,128]{1,0:T(8,128)S(1)} %get-tuple-element.9.outer, bf16[2,320,256]{2,1,0:T(8,128)(2,1)S(1)} %get-tuple-element.10.tables), custom_call_target="tpu_custom_call" | custom-call | tf_op jit(solution)/shard_map/make_children/pallas_call | solution.py:600

commit v8 on v7

--- a/solution.py
+++ b/solution.py
@@ -486,7 +486,7 @@
 
 
 def child_kernel(inner, outer, tables, out_hbm, flat, out, store_sem):
-    cuts = (0, 256, DEVICES * SLOTS)
+    cuts = (0, 640, DEVICES * SLOTS)
 
     def unpack(part):
         first, slots = cuts[part], cuts[part + 1] - cuts[part]

time: 25 us -> 25 us (level)
  no operation moved by 1% of the time
where the time goes in v8:
time: 25 us; the launch traced here: 24.9 us
  Pallas kernels  24.9 us (100%)
    pallas_call x1, Pallas kernels, on_device(): pl.pallas_call(step_kernel, out_shape=(jax.ShapeDtypeStruct((INNER, slots...  22.5 us
    pallas_call x1, Pallas kernels, on_device(): pl.pallas_call(child_kernel, out_shape=jax.ShapeDtypeStruct((768, slots),...  2.37 us

profile of v8, /device:TPU:1, one launch (start us, length us, event | category | flops | bytes accessed | tf_op | source)
XLA Modules:
  0.0 24.9 jit_solution(2630037977927164451)
XLA Ops:
  0.0 22.5 %step_and_migrate.1 = (f32[112,1024]{1,0:T(8,128)S(1)}, f32[1024,128]{1,0:T(8,128)S(1)}, bf16[2,320,256]{2,1,0:T(8,128)(2,1)S(1)}) custom-call(f32[192,512]{1,0:T(8,128)} %bitcast.5, s32[4,512]{1,0:T(4,128)} %neighbours_in.1, f32[1,512]{1,0:T(1,128)} %bitcast.6, s32[1,512]{1,0:T(1,128)} %bitcast.7, s32[1,512]{1,0:T(1,128)} %bitcast.8, ...), custom_call_target="tpu_custom_call" | custom-call | tf_op jit(solution)/shard_map/step_and_migrate/pallas_call | solution.py:548
  22.5 2.4 %make_children.1 = f32[768,1024]{1,0:T(8,128)} custom-call(f32[112,1024]{1,0:T(8,128)S(1)} %get-tuple-element.8.inner, f32[1024,128]{1,0:T(8,128)S(1)} %get-tuple-element.9.outer, bf16[2,320,256]{2,1,0:T(8,128)(2,1)S(1)} %get-tuple-element.10.tables), custom_call_target="tpu_custom_call" | custom-call | tf_op jit(solution)/shard_map/make_children/pallas_call | solution.py:600
